TPU v7x, 1024 devices: a whole 4x8x16 slice. The times are simulated.
1024 devices in a mesh: lat: 16 (over z), lev: 16 (over y, core), rep: 4 (over x).
Axes of the slice: x: 4, y: 8, z: 16, core: 2. Of those that a mesh axis runs over, the one named last changes fastest.
Arguments:
- spectral: bfloat16 [320, 641, 2, 2, 64], P('lat', None, None, None, 'lev'), may hold values from -0.4375 to 0.4375
- legendre: bfloat16 [320, 641, 960], P('lat', None, 'rep'), may hold values from -0.25 to 0.25
- pair_table: int32 [320, 2], replicated, may hold values from 640 to 1279, as said below
- weight_in: bfloat16 [128, 256], replicated, may hold values from -0.5 to 0.5
- bias_in: float32 [256], replicated, may hold values from -3 to 3
- weight_out: bfloat16 [256, 128], replicated, may hold values from -0.375 to 0.375
- cotangent: bfloat16 [128, 3686400], P(None, ('lat', 'lev', 'rep')), may hold values from -0.0078125 to 0.0078125
Outputs:
- grad_w_in: float32 [128, 256], replicated
- grad_b_in: float32 [256], replicated
- grad_w_out: float32 [256, 128], replicated
- grad_b_out: float32 [128], replicated
Inputs may be any that keep to these rules, and one draw needn't show every extreme that they name: `pair_table`: row p holds a wavenumber m and 1919 - m, in either order; every wavenumber from 640 to 1279 appears exactly once in the table.
All inputs are finite; a program needn't handle non-finite values.
Results may differ from a plain program's by a relative error of at most 0.0072.
Values may be sent and summed in bfloat16 or wider, within the bound.
A program may use at most 64 MiB of HBM per device.

v0:
```python
import math

import jax
import jax.numpy as jnp
from jax import lax
from jax.sharding import PartitionSpec as P

TRUNCATION_PLUS = 1280
LON = 3840


def dft_table(m_slots, lon_ids, lon_total):
    product = m_slots[:, None] * lon_ids[None, :] % lon_total
    angle = product.astype(jnp.float32) * (2.0 * math.pi / lon_total)
    return jnp.stack([2.0 * jnp.cos(angle), -2.0 * jnp.sin(angle)]).astype(jnp.bfloat16)


def body(spectral, legendre, pair_table, weight_in, bias_in, weight_out, cotangent):
    pairs_dev = legendre.shape[0]
    prow_count = legendre.shape[1]
    lat_index = lax.axis_index("lat")
    lev_index = lax.axis_index("lev")
    lev_count = lax.axis_size("lev")
    local_pair_list = lax.dynamic_slice_in_dim(pair_table, lat_index * pairs_dev, pairs_dev, 0)
    row_ids = jnp.arange(prow_count, dtype=jnp.int32)
    row_count = TRUNCATION_PLUS - local_pair_list[:, 0]
    lower_mask = (row_ids[None, :] < row_count[:, None]).astype(jnp.bfloat16)
    masked = spectral * lower_mask[:, :, None, None, None]
    halves = jnp.stack([masked, spectral - masked], axis=2)
    fourier = jnp.einsum("prl,prwfek->fkepwl", legendre, halves, preferred_element_type=jnp.float32)
    field_count = fourier.shape[0]
    lev_dev = fourier.shape[1]
    item_count = field_count * lev_dev
    fourier = fourier.astype(jnp.bfloat16).reshape(item_count, 2, 2 * pairs_dev, legendre.shape[2])
    transposed = lax.all_to_all(fourier, "lat", split_axis=3, concat_axis=2, tiled=True)
    lat_dev = transposed.shape[3]
    lon_dev = LON // lev_count
    m_slots = pair_table.reshape(-1)
    own_lon = lev_index * lon_dev + jnp.arange(lon_dev, dtype=jnp.int32)
    own_table = dft_table(m_slots, own_lon, LON)
    gathered = jnp.einsum(
        "irsj,rsn->ijn",
        lax.all_gather(transposed, "lev", axis=0, tiled=True),
        own_table,
        preferred_element_type=jnp.float32,
    ).astype(jnp.bfloat16)
    gathered = gathered.reshape(lev_count, field_count, lev_dev, lat_dev * lon_dev).transpose(
        1, 0, 2, 3
    )
    inputs = gathered.reshape(field_count * lev_count * lev_dev, lat_dev * lon_dev)
    preact = (
        jnp.einsum("fh,fc->hc", weight_in, inputs, preferred_element_type=jnp.float32)
        + bias_in[:, None]
    )
    sigmoid_z = jax.nn.sigmoid(preact)
    activation = (preact * sigmoid_z).astype(jnp.bfloat16)
    activation_gradient = jnp.dot(weight_out, cotangent, preferred_element_type=jnp.float32)
    grad_pre = (activation_gradient * sigmoid_z * (1.0 + preact * (1.0 - sigmoid_z))).astype(
        jnp.bfloat16
    )
    grad_w1 = jnp.einsum("fc,hc->fh", inputs, grad_pre, preferred_element_type=jnp.float32)
    grad_b1 = jnp.sum(grad_pre.astype(jnp.float32), axis=1)
    grad_w2 = jnp.einsum("hc,fc->hf", activation, cotangent, preferred_element_type=jnp.float32)
    grad_b2 = jnp.sum(cotangent.astype(jnp.float32), axis=1)
    summed = lax.psum((grad_w1, grad_b1, grad_w2, grad_b2), ("lat", "lev", "rep"))
    return (summed[0], summed[1], summed[2], summed[3])


def solution(mesh):
    in_specs = (
        P("lat", None, None, None, "lev"),
        P("lat", None, "rep"),
        P(),
        P(),
        P(),
        P(),
        P(None, ("lat", "lev", "rep")),
    )
    out_specs = (P(), P(), P(), P())
    return jax.shard_map(body, mesh=mesh, in_specs=in_specs, out_specs=out_specs, check_vma=False)
```

profile of v0, /device:TPU:1, one launch (start us, length us, event | category | flops | bytes accessed | tf_op | source)
XLA Modules:
  0.0 606.5 jit_solution(9903540960133746242)
XLA Ops:
  7.2 0.0 all-gather.2.cloned.1.call-start
  7.2 0.8 constant_dynamic-slice_fusion
  8.0 0.1 fusion.23
  8.1 1.4 multiply_bitcast_fusion
  9.5 4.4 fusion.9
  13.9 0.3 copy.28
  14.2 1.5 copy.29
  15.7 1.4 reshape.189
  17.1 33.7 %all_to_all.18 = bf16[16,2,4800]{2,1,0:T(2,128)(2,1)S(1)} all-to-all(bf16[16,2,4800]{2,1,0:T(2,128)(2,1)S(1)} %reshape.189), channel_id=1, replica_groups=mesh['lat'=16,'lev'=16,'rep'=4] {'lat'}, dimensions={0} | all-to-all | bytes 614400 | tf_op jit(solution)/shard_map/all_to_all | solution.py:35
  50.8 1.1 reshape.190
  51.9 0.3 copy.31
  52.2 1.9 all_to_all.16
  54.1 0.0 all-gather.2.cloned.1.call-update
  54.1 0.2 all-reduce.4.cloned.1.call-start
  54.3 0.1 copy.32
  54.5 0.1 mul.98
  54.6 3.0 multiply_convert_fusion.3
  57.7 49.1 %all-gather.2.cloned.1.call-done = bf16[128,2,640,15]{2,0,1,3:T(8,128)(2,1)} async-done(((bf16[8,2,640,15]{2,0,1,3:T(8,128)(2,1)}), bf16[128,2,640,15]{2,0,1,3:T(8,128)(2,1)}) %all-gather.2.cloned.1.call-update) | async-done | bytes 4915216 | tf_op jit(solution)/shard_map/all_gather | solution.py:43
  106.8 4.0 bitcast_convert_fusion
  110.8 1.4 copy.33
  112.2 1.8 reshape.184
  114.0 0.3 copy.34
  114.4 0.5 reshape.185
  114.8 0.7 fusion.3
  115.5 1.8 fusion.5
  117.4 1.6 convert_reduce_fusion
  119.0 1.1 fusion.27
  120.1 0.5 convert_reduce_fusion.1
  120.6 125.2 %all-reduce = (f32[256]{0:T(256)}, f32[128]{0:T(128)}) all-reduce(f32[256]{0:T(256)S(1)} %get-tuple-element.12, f32[128]{0:T(128)S(1)} %convert_reduce_fusion.1), channel_id=1, replica_groups=mesh['lat'=16,'lev'=16,'rep'=4] {'lat','lev','rep'}, use_global_device_ids=true, to_apply=%region_2.3 | all-reduce | flops 384 | bytes 3072 | tf_op jit(solution)/shard_map/psum | solution.py:65
  245.9 350.7 %all-reduce.4.cloned.1.call-done = (f32[128,256]{1,0:T(8,128)}, f32[256,128]{1,0:T(8,128)}) async-done(((f32[128,256]{1,0:T(8,128)}, f32[256,128]{1,0:T(8,128)}), (f32[128,256]{1,0:T(8,128)}, f32[256,128]{1,0:T(8,128)})) %all-reduce.4.cloned.1.call-update) | async-done | bytes 262160 | tf_op jit(solution)/shard_map/psum | solution.py:65
  596.5 1.6 copy.40
  598.1 1.6 copy.41
  (13 shorter events, 0.1 us)
Async XLA Ops:
  7.2 110.2 %copy-start = (bf16[256,128]{1,0:T(8,128)(2,1)S(1)}, bf16[256,128]{1,0:T(8,128)(2,1)}, u32[]{:S(2)}) copy-start(bf16[256,128]{1,0:T(8,128)(2,1)} %param.12) | copy-start | bytes 196612
  7.2 99.6 %all-gather.2.cloned.1.call-start = ((), (), s32[]{:S(2)}) async-start(), calls=%async_computation.1 | async-start | bytes 5222400 | tf_op jit(solution)/shard_map/all_gather | solution.py:43
  15.7 38.7 %copy-start.3 = (s32[320,2]{0,1:T(2,128)S(1)}, s32[320,2]{0,1:T(2,128)}, u32[]{:S(2)}) copy-start(s32[320,2]{0,1:T(2,128)} %param.9) | copy-start | bytes 7684
  54.1 542.4 %all-reduce.4.cloned.1.call-start = ((), (), s32[]{:S(2)}) async-start(), calls=%async_computation.2 | async-start | bytes 524288 | tf_op jit(solution)/shard_map/psum | solution.py:65
  110.8 4.0 copy-start.2
  110.8 4.0 copy-start.4
  114.3 1.2 copy-start.1
Sparse Core Ops, SparseCore 0:
  54.2 52.5 all-gather.1
  120.3 476.2 all-reduce.3
where the time goes:
time: 608 us; the launch traced here: 606 us
  waiting for transfers between devices  400 us (66%)
  blocking collectives  159 us (26%)
  local copies, waits for them, and re-layouts  14.6 us (2%)
  between operations  14.2 us (2%)
  matrix products  13.6 us (2%)
    psum x1, waiting for transfers between devices, body(): lax.psum((grad_w1, grad_b1, grad_w2, grad_b2), ('lat', 'lev', 'rep'))  351 us
    psum x1, blocking collectives, body(): lax.psum((grad_w1, grad_b1, grad_w2, grad_b2), ('lat', 'lev', 'rep'))  125 us
    all_gather x1, waiting for transfers between devices, body(): lax.all_gather(transposed, 'lev', axis=0, tiled=True)  49.1 us
    all_to_all x1, blocking collectives, body(): lax.all_to_all(fourier, 'lat', split_axis=3, concat_axis=2, tiled=True)  33.7 us
  transfers between devices with their start and end apart: 2, of which 2 were waited for; matrix products, arithmetic and copies ran while one was open for 1% of the time, Pallas kernels for 0%

commit v1 on v0

--- a/solution.py
+++ b/solution.py
@@ -1,12 +1,186 @@
+import functools
 import math
 
 import jax
 import jax.numpy as jnp
 from jax import lax
+from jax.experimental import pallas as pl
+from jax.experimental.pallas import tpu as pltpu
 from jax.sharding import PartitionSpec as P
 
 TRUNCATION_PLUS = 1280
 LON = 3840
+LANES = 128
+ROWS = 9
+MESH = pl.DeviceIdType.MESH
+
+
+def greet(targets):
+    barrier = pltpu.get_barrier_semaphore()
+    for target in targets:
+        pl.semaphore_signal(barrier, inc=1, device_id=target, device_id_type=MESH)
+    pl.semaphore_wait(barrier, len(targets))
+
+
+def push(src, dst, sems, slot, target):
+    copy = pltpu.make_async_remote_copy(
+        src_ref=src,
+        dst_ref=dst,
+        send_sem=sems.at[0, slot],
+        recv_sem=sems.at[1, slot],
+        device_id=target,
+        device_id_type=MESH,
+    )
+    copy.start()
+    return copy
+
+
+def wait_all(copies):
+    for copy in copies:
+        copy.wait()
+
+
+def sum_kernel(
+    n_x, n_y, n_z,
+    w1_ref, b1_ref, w2_ref, b2_ref,
+    o1_ref, ob1_ref, o2_ref, ob2_ref,
+    part, recv_c, sum_c, recv_x, sum_x, recv_y, all_z, total, sems,
+):
+    x = lax.axis_index("rep")
+    lev = lax.axis_index("lev")
+    z = lax.axis_index("lat")
+    core = lax.rem(lev, 2)
+    y = lev // 2
+    partner = {"lev": lev + 1 - 2 * core}
+    x_peers = [lax.rem(x + d, n_x) for d in range(1, n_x)]
+    y_peers = [lax.rem(y + d, n_y) for d in range(1, n_y)]
+    z_peers = [lax.rem(z + d, n_z) for d in range(1, n_z)]
+    x_dev = [{"rep": v} for v in x_peers]
+    y_dev = [{"lev": v * 2 + core} for v in y_peers]
+    z_dev = [{"lat": v} for v in z_peers]
+    greet([partner] + x_dev + y_dev + z_dev)
+
+    chunks = part.shape[0]
+    half = chunks // 2
+    quarter = chunks // 4
+    for q in range(chunks):
+        if q < quarter:
+            block = w1_ref[8 * q : 8 * q + 8, :LANES]
+        elif q < half:
+            block = w1_ref[8 * (q - quarter) : 8 * (q - quarter) + 8, LANES:]
+        else:
+            block = w2_ref[8 * (q - half) : 8 * (q - half) + 8, :]
+        part[q, 0:8, :] = block
+        if q < 2:
+            part[q, 8:9, :] = b1_ref[q : q + 1, :]
+        elif q == 2:
+            part[q, 8:9, :] = b2_ref[...]
+        else:
+            part[q, 8:9, :] = jnp.zeros((1, LANES), jnp.float32)
+
+    base = 0
+    copies = [push(part.at[pl.ds((1 - core) * half, half)], recv_c, sems, base, partner)]
+    base += 1
+    wait_all(copies)
+    sum_c[...] = part[pl.ds(core * half, half)] + recv_c[...]
+
+    copies = []
+    for d in range(1, n_x):
+        copies.append(
+            push(sum_c.at[pl.ds(x_peers[d - 1] * n_y, n_y)], recv_x.at[d - 1], sems, base, x_dev[d - 1])
+        )
+        base += 1
+    wait_all(copies)
+    value = sum_c[pl.ds(x * n_y, n_y)]
+    for d in range(1, n_x):
+        value = value + recv_x[d - 1]
+    sum_x[...] = value
+
+    copies = []
+    for d in range(1, n_y):
+        copies.append(push(sum_x.at[y_peers[d - 1]], recv_y.at[d - 1], sems, base, y_dev[d - 1]))
+        base += 1
+    wait_all(copies)
+    value = sum_x[y]
+    for d in range(1, n_y):
+        value = value + recv_y[d - 1]
+    all_z[z] = value
+
+    copies = []
+    for d in range(1, n_z):
+        copies.append(push(all_z.at[z], all_z.at[z], sems, base, z_dev[d - 1]))
+        base += 1
+    wait_all(copies)
+    value = all_z[0]
+    for s in range(1, n_z):
+        value = value + all_z[s]
+    mine = (core * n_x + x) * n_y + y
+    total[mine] = value
+
+    copies = []
+    for d in range(1, n_y):
+        copies.append(push(total.at[mine], total.at[mine], sems, base, y_dev[d - 1]))
+        base += 1
+    wait_all(copies)
+    row = total.at[pl.ds((core * n_x + x) * n_y, n_y)]
+    copies = []
+    for d in range(1, n_x):
+        copies.append(push(row, row, sems, base, x_dev[d - 1]))
+        base += 1
+    wait_all(copies)
+    side = total.at[pl.ds(core * half, half)]
+    copies = [push(side, side, sems, base, partner)]
+    base += 1
+    wait_all(copies)
+
+    for q in range(chunks):
+        block = total[q, 0:8, :]
+        if q < quarter:
+            o1_ref[8 * q : 8 * q + 8, :LANES] = block
+        elif q < half:
+            o1_ref[8 * (q - quarter) : 8 * (q - quarter) + 8, LANES:] = block
+        else:
+            o2_ref[8 * (q - half) : 8 * (q - half) + 8, :] = block
+        if q < 2:
+            ob1_ref[q : q + 1, :] = total[q, 8:9, :]
+        elif q == 2:
+            ob2_ref[...] = total[q, 8:9, :]
+
+
+def sum_over_devices(w1, b1, w2, b2):
+    n_z = lax.axis_size("lat")
+    n_y = lax.axis_size("lev") // 2
+    n_x = lax.axis_size("rep")
+    feat, hid = w1.shape
+    chunks = 2 * n_x * n_y
+    f32 = jnp.float32
+    copies = 2 + 2 * (n_x - 1) + 2 * (n_y - 1) + (n_z - 1)
+    vmem = pl.BlockSpec(memory_space=pltpu.VMEM)
+    o1, ob1, o2, ob2 = pl.pallas_call(
+        functools.partial(sum_kernel, n_x, n_y, n_z),
+        out_shape=(
+            jax.ShapeDtypeStruct((feat, hid), f32),
+            jax.ShapeDtypeStruct((2, LANES), f32),
+            jax.ShapeDtypeStruct((hid, feat), f32),
+            jax.ShapeDtypeStruct((1, LANES), f32),
+        ),
+        in_specs=[vmem] * 4,
+        out_specs=(vmem,) * 4,
+        scratch_shapes=[
+            pltpu.VMEM((chunks, ROWS, LANES), f32),
+            pltpu.VMEM((chunks // 2, ROWS, LANES), f32),
+            pltpu.VMEM((chunks // 2, ROWS, LANES), f32),
+            pltpu.VMEM((n_x - 1, n_y, ROWS, LANES), f32),
+            pltpu.VMEM((n_y, ROWS, LANES), f32),
+            pltpu.VMEM((n_y - 1, ROWS, LANES), f32),
+            pltpu.VMEM((n_z, ROWS, LANES), f32),
+            pltpu.VMEM((chunks, ROWS, LANES), f32),
+            pltpu.SemaphoreType.DMA((2, copies)),
+        ],
+        compiler_params=pltpu.CompilerParams(collective_id=0, has_side_effects=True),
+        name="sum_over_devices",
+    )(w1, b1.reshape(2, LANES), w2, b2.reshape(1, LANES))
+    return o1, ob1.reshape(hid), o2, ob2.reshape(feat)
 
 
 def dft_table(m_slots, lon_ids, lon_total):
@@ -62,8 +236,7 @@
     grad_b1 = jnp.sum(grad_pre.astype(jnp.float32), axis=1)
     grad_w2 = jnp.einsum("hc,fc->hf", activation, cotangent, preferred_element_type=jnp.float32)
     grad_b2 = jnp.sum(cotangent.astype(jnp.float32), axis=1)
-    summed = lax.psum((grad_w1, grad_b1, grad_w2, grad_b2), ("lat", "lev", "rep"))
-    return (summed[0], summed[1], summed[2], summed[3])
+    return sum_over_devices(grad_w1, grad_b1, grad_w2, grad_b2)
 
 
 def solution(mesh):

time: 608 us -> 175 us (0.29)
  waiting for transfers between devices: 400 us -> 48.4 us
  blocking collectives: 159 us -> 33.7 us
  Pallas kernels: 0 us -> 41 us
    psum x1 -> x0, waiting for transfers between devices: 351 us -> none  [body(): lax.psum((grad_w1, grad_b1, grad_w2, grad_b2), ('lat', 'lev', 'rep'))]
    psum x1 -> x0, blocking collectives: 125 us -> none  [body(): lax.psum((grad_w1, grad_b1, grad_w2, grad_b2), ('lat', 'lev', 'rep'))]
    pallas_call x0 -> x1, Pallas kernels: none -> 41 us  [sum_over_devices(): pl.pallas_call(functools.partial(sum_kernel, n_x, n_y, n_z), out_shape=(j...]
  transfers between devices with their start and end apart: 2 -> 1, of which waited for: 2 -> 1; matrix products, arithmetic and copies ran while one was open for 1% -> 2% of each run, Pallas kernels for 0% -> 0%
where the time goes in v1:
time: 175 us; the launch traced here: 174 us
  waiting for transfers between devices  48.4 us (28%)
  Pallas kernels  41 us (23%)
  blocking collectives  33.7 us (19%)
  local copies, waits for them, and re-layouts  17 us (10%)
  between operations  14.3 us (8%)
  matrix products  14.2 us (8%)
  other arithmetic  5.51 us (3%)
    all_gather x1, waiting for transfers between devices, body(): lax.all_gather(transposed, 'lev', axis=0, tiled=True)  48.4 us
    pallas_call x1, Pallas kernels, sum_over_devices(): pl.pallas_call(functools.partial(sum_kernel, n_x, n_y, n_z), out_shape=(j...  41 us
    all_to_all x1, blocking collectives, body(): lax.all_to_all(fourier, 'lat', split_axis=3, concat_axis=2, tiled=True)  33.7 us
    unnamed x19, local copies, waits for them, and re-layouts  8.18 us
    dot_general x1, matrix products, body(): jnp.einsum('prl,prwfek->fkepwl', legendre, halves, preferred_element_type...  4.44 us
    dot_general x1, matrix products, body(): jnp.einsum('irsj,rsn->ijn', lax.all_gather(transposed, 'lev', axis=0, til...  3.95 us
  transfers between devices with their start and end apart: 1, of which 1 were waited for; matrix products, arithmetic and copies ran while one was open for 2% of the time, Pallas kernels for 0%

profile of v1, /device:TPU:1, one launch (start us, length us, event | category | flops | bytes accessed | tf_op | source)
XLA Modules:
  0.0 174.1 jit_solution(2503394785516587131)
XLA Ops:
  7.2 0.0 all-gather.2.cloned.1.call-start
  7.2 0.8 constant_dynamic-slice_fusion
  8.0 0.1 fusion.23
  8.1 1.4 multiply_bitcast_fusion
  9.5 4.4 %fusion.9 = bf16[2,4,2,20,2,240]{5,1,2,0,4,3:T(4,128)(2,1)S(1)} fusion(bf16[20,641,240]{2,1,0:T(8,128)(2,1)} %param.8, bf16[20,641,1,2,2,4]{1,5,4,3,2,0:T(4,128)(2,1)S(1)} %get-tuple-element.13, bf16[20,641,1,2,2,4]{1,5,4,3,2,0:T(4,128)(2,1)S(1)} %get-tuple-element.12), kind=kOutput, calls=%fused_computation.14 | convolution fusion | flops 198709760 | bytes 7281280 | tf_op jit(solution)/shard_map/prl,prwfek->fkepwl/dot_general | solution.py:204
  13.9 0.3 copy.28
  14.2 1.5 copy.29
  15.7 1.4 reshape.205
  17.1 33.7 %all_to_all.18 = bf16[16,2,4800]{2,1,0:T(2,128)(2,1)S(1)} all-to-all(bf16[16,2,4800]{2,1,0:T(2,128)(2,1)S(1)} %reshape.205), channel_id=1, replica_groups=mesh['lat'=16,'lev'=16,'rep'=4] {'lat'}, dimensions={0} | all-to-all | bytes 614400 | tf_op jit(solution)/shard_map/all_to_all | solution.py:209
  50.8 1.1 reshape.206
  51.9 0.3 copy.31
  52.2 1.8 %all_to_all.16 = bf16[8,2,640,15]{2,0,1,3:T(8,128)(2,1)} reshape(bf16[8,2,16,40,15]{3,2,0,1,4:T(8,128)(2,1)S(1)} %copy.31) | data formatting | bytes 614400 | tf_op jit(solution)/shard_map/all_to_all | solution.py:209
  54.0 0.0 all-gather.2.cloned.1.call-update
  54.1 0.1 copy.32
  54.2 0.1 mul.98
  54.4 1.0 convert_reduce_fusion.1
  55.4 3.0 %multiply_convert_fusion.3 = (bf16[1,640,240]{1,2,0:T(8,128)(2,1)S(1)}, bf16[1,640,240]{1,2,0:T(8,128)(2,1)S(1)}) fusion(s32[240]{0:T(256)S(1)} %iota_add_fusion, s32[640]{0:T(1024)S(1)} %mul.98), kind=kLoop, calls=%fused_computation.27 | loop fusion | flops 1996800 | bytes 617920 | tf_op jit(solution)/shard_map/convert
  58.4 48.4 %all-gather.2.cloned.1.call-done = bf16[128,2,640,15]{2,0,1,3:T(8,128)(2,1)} async-done(((bf16[8,2,640,15]{2,0,1,3:T(8,128)(2,1)}), bf16[128,2,640,15]{2,0,1,3:T(8,128)(2,1)}) %all-gather.2.cloned.1.call-update) | async-done | bytes 4915216 | tf_op jit(solution)/shard_map/all_gather | solution.py:217
  106.8 4.0 %bitcast_convert_fusion = bf16[128,15,240]{0,2,1:T(8,128)(2,1)S(1)} fusion(bf16[128,2,640,15]{2,0,1,3:T(8,128)(2,1)} %all-gather.2.cloned.1.call-done, bf16[1,640,240]{1,2,0:T(8,128)(2,1)S(1)} %get-tuple-element.15, bf16[1,640,240]{1,2,0:T(8,128)(2,1)S(1)} %get-tuple-element.14), kind=kOutput, calls=%fused_computation.10 | convolution fusion | flops 1180416000 | bytes 6451200 | tf_op jit(solution)/shard_map/irsj,rsn->ijn/dot_general | solution.py:215
  110.8 1.5 copy.33
  112.3 1.8 %reshape.196 = bf16[16,2,4,3600]{3,2,1,0:T(4,128)(2,1)S(1)} reshape(bf16[128,15,240]{2,1,0:T(8,128)(2,1)S(1)} %copy.33) | data formatting | bytes 1843200 | tf_op jit(solution)/shard_map/reshape | solution.py:221
  114.1 0.3 copy.34
  114.5 0.5 reshape.197
  115.0 0.7 fusion.3
  115.7 1.9 %fusion.5.w2_ref = f32[256,128]{1,0:T(8,128)} fusion(bf16[128,3600]{0,1:T(8,128)(2,1)S(1)} %copy-done.2, f32[256,3600]{0,1:T(8,128)S(1)} %fusion.3), kind=kOutput, calls=%fused_computation.12 | convolution fusion | flops 240537600 | bytes 4739072 | tf_op jit(solution)/shard_map/hc,fc->hf/dot_general | solution.py:237
  117.5 2.2 %convert_reduce_fusion = (f32[256]{0:T(256)}, bf16[256,3600]{0,1:T(8,128)(2,1)S(1)}) fusion(f32[256,3600]{0,1:T(8,128)S(1)} %fusion.3, bf16[256,128]{1,0:T(8,128)(2,1)S(1)} %copy-done, bf16[128,3600]{0,1:T(8,128)(2,1)S(1)} %copy-done.2), kind=kOutput, calls=%fused_computation.8 | convolution fusion | flops 246066944 | bytes 6517760 | tf_op jit(solution)/shard_map/dot_general | solution.py:231
  119.7 1.1 fusion.27.w1_ref
  120.8 41.0 %sum_over_devices.1 = (f32[128,256]{1,0:T(8,128)}, f32[2,128]{1,0:T(2,128)}, f32[256,128]{1,0:T(8,128)}, f32[1,128]{1,0:T(1,128)}) custom-call(f32[128,256]{1,0:T(8,128)} %fusion.27.w1_ref, f32[2,128]{1,0:T(2,128)} %bitcast.55, f32[256,128]{1,0:T(8,128)} %fusion.5.w2_ref, f32[1,128]{1,0:T(1,128)} %bitcast.54), custom_call_target="tpu_custom_call" | custom-call | tf_op jit(solution)/shard_map/sum_over_devices/pallas_call | solution.py:159
  161.8 1.6 copy.42
  163.4 1.2 copy.43
  164.6 1.6 copy.44
  166.2 1.1 copy.45
  (14 shorter events, 0.1 us)
Async XLA Ops:
  7.2 110.4 %copy-start = (bf16[256,128]{1,0:T(8,128)(2,1)S(1)}, bf16[256,128]{1,0:T(8,128)(2,1)}, u32[]{:S(2)}) copy-start(bf16[256,128]{1,0:T(8,128)(2,1)} %param.12) | copy-start | bytes 196612
  7.2 99.6 %all-gather.2.cloned.1.call-start = ((), (), s32[]{:S(2)}) async-start(), calls=%async_computation.1 | async-start | bytes 5222400 | tf_op jit(solution)/shard_map/all_gather | solution.py:217
  15.7 38.4 %copy-start.4 = (s32[320,2]{0,1:T(2,128)S(1)}, s32[320,2]{0,1:T(2,128)}, u32[]{:S(2)}) copy-start(s32[320,2]{0,1:T(2,128)} %param.9) | copy-start | bytes 7684
  15.7 38.7 %copy-start.1 = (bf16[128,3600]{0,1:T(8,128)(2,1)S(1)}, bf16[128,3600]{0,1:T(8,128)(2,1)}, u32[]{:S(2)}) copy-start(bf16[128,3600]{0,1:T(8,128)(2,1)} %param.13) | copy-start | bytes 2764804
  110.7 4.2 %copy-start.3 = (bf16[128,256]{1,0:T(8,128)(2,1)S(1)}, bf16[128,256]{1,0:T(8,128)(2,1)}, u32[]{:S(2)}) copy-start(bf16[128,256]{1,0:T(8,128)(2,1)} %param.10) | copy-start | bytes 196612
  110.7 4.2 %copy-start.5 = (f32[256]{0:T(256)S(1)}, f32[256]{0:T(256)}, u32[]{:S(2)}) copy-start(f32[256]{0:T(256)} %param.11) | copy-start | bytes 3076
  114.5 1.2 copy-start.2
Sparse Core Ops, SparseCore 0:
  54.2 52.5 all-gather.1

commit v2 on v1

v2 whole, which is shorter than its diff:
```python
import functools
import math

import jax
import jax.numpy as jnp
from jax import lax
from jax.experimental import pallas as pl
from jax.experimental.pallas import tpu as pltpu
from jax.sharding import PartitionSpec as P

TRUNCATION_PLUS = 1280
LON = 3840
LANES = 128
ROWS = 9
MESH = pl.DeviceIdType.MESH


GROUPS = 4
SHARD = 8


def greet(targets):
    barrier = pltpu.get_barrier_semaphore()
    for target in targets:
        pl.semaphore_signal(barrier, inc=1, device_id=target, device_id_type=MESH)
    pl.semaphore_wait(barrier, len(targets))


def push(src, dst, send_sem, recv_sem, target):
    copy = pltpu.make_async_remote_copy(
        src_ref=src,
        dst_ref=dst,
        send_sem=send_sem,
        recv_sem=recv_sem,
        device_id=target,
        device_id_type=MESH,
    )
    copy.start()
    return copy


def wait_all(copies):
    for copy in copies:
        copy.wait()


def nt(a, b):
    return lax.dot_general(a, b, (((1,), (1,)), ((), ())), preferred_element_type=jnp.float32)


def nn(a, b):
    return jnp.dot(a, b, preferred_element_type=jnp.float32)


def gradient_kernel(
    n_x, n_y, n_z,
    f_ref, trig_ref, cot_ref, win_ref, bias_ref, wout_ref,
    out_ref,
    spread, grid, wperm, wt, biasb, cotpad, acc1, acc2, accb1, accb2,
    part, recv_c, sum_c, recv_x, sum_x, recv_y, all_z, total,
    z_send, z_recv, y_send, y_recv, p_send, p_recv, r_send, r_recv,
):
    x = lax.axis_index("rep")
    lev = lax.axis_index("lev")
    z = lax.axis_index("lat")
    core = lax.rem(lev, 2)
    y = lev // 2
    partner = {"lev": lev + 1 - 2 * core}
    x_peers = [lax.rem(x + d, n_x) for d in range(1, n_x)]
    y_peers = [lax.rem(y + d, n_y) for d in range(1, n_y)]
    z_peers = [lax.rem(z + d, n_z) for d in range(1, n_z)]
    x_dev = [{"rep": v} for v in x_peers]
    y_dev = [{"lev": v * 2 + core} for v in y_peers]
    z_dev = [{"lat": v} for v in z_peers]
    greet([partner] + x_dev + y_dev + z_dev)

    rows = f_ref.shape[1]
    mine_block = spread.at[lev, pl.ds(pl.multiple_of(z * rows, 16), rows)]
    own = pltpu.make_async_copy(f_ref.at[z], mine_block, z_recv.at[z])
    own.start()
    order = []
    for d in range(1, n_z // 2 + 1):
        order.append(d)
        if d != n_z - d:
            order.append(n_z - d)
    z_copies = []
    for d in order:
        z_copies.append(
            push(f_ref.at[z_peers[d - 1]], mine_block, z_send.at[d - 1], z_recv.at[z], z_dev[d - 1])
        )

    w32 = win_ref[...].astype(jnp.float32)
    levels = w32.shape[0] // SHARD
    for v in range(levels):
        for f in range(2):
            a = v * SHARD + f * 4
            b = f * levels * 4 + v * 4
            wperm[a : a + 4, :] = w32[b : b + 4, :]
    wt[...] = wperm[...].T.astype(jnp.bfloat16)
    biasb[...] = jnp.broadcast_to(bias_ref[...], (LANES, biasb.shape[0])).T
    cotpad[...] = jnp.zeros(cotpad.shape, cotpad.dtype)
    acc1[...] = jnp.zeros(acc1.shape, acc1.dtype)
    acc2[...] = jnp.zeros(acc2.shape, acc2.dtype)
    accb1[...] = jnp.zeros(accb1.shape, accb1.dtype)
    accb2[...] = jnp.zeros(accb2.shape, accb2.dtype)

    per = n_z // GROUPS
    span = per * rows
    offsets = [0, 1, GROUPS - 1, 2]
    group = [lax.rem(z // per + o, GROUPS) for o in offsets]
    right = y_dev[0]
    left = y_dev[n_y - 2]
    half_way = n_y // 2
    y_copies = {}
    p_copies = []

    def region(origin, b):
        start = pl.multiple_of(group[b] * span, 16)
        return spread.at[origin * 2 + core, pl.ds(start, span)]

    def send_y(b, way, step, origin):
        ref = region(origin, b)
        slot = (b * 2 + way) * half_way + step - 1
        y_copies[b, way, step] = push(
            ref, ref, y_send.at[slot], y_recv.at[slot], right if way == 0 else left
        )

    def send_p(b, slot, origin):
        ref = region(origin, b)
        at = b * 2 * n_y + slot
        p_copies.append(push(ref, ref, p_send.at[at], p_recv.at[at], partner))

    last = [[half_way if b % 2 == 0 else half_way - 1, half_way if b % 2 else half_way - 1] for b in range(GROUPS)]
    for tick in range(GROUPS + half_way):
        for b in range(GROUPS):
            step = tick - b
            if step == 0:
                for i in range(per):
                    src = group[b] * per + i
                    block = spread.at[lev, pl.ds(pl.multiple_of(src * rows, 16), rows)]
                    pltpu.make_async_remote_copy(
                        src_ref=block,
                        dst_ref=block,
                        send_sem=z_send.at[0],
                        recv_sem=z_recv.at[src],
                        device_id=partner,
                        device_id_type=MESH,
                    ).wait_recv()
                send_y(b, 0, 1, y)
                send_y(b, 1, 1, y)
                send_p(b, 0, y)
            elif step > 0:
                for way in range(2):
                    if step > last[b][way]:
                        continue
                    origin = lax.rem(y + (n_y - step if way == 0 else step), n_y)
                    y_copies[b, way, step].wait_recv()
                    if step < last[b][way]:
                        send_y(b, way, step + 1, origin)
                    send_p(b, 1 + way * half_way + step - 1, origin)
    for copy in z_copies:
        copy.wait_send()
    for copy in y_copies.values():
        copy.wait_send()
    wait_all(p_copies)

    lat = grid.shape[0]
    lons = cot_ref.shape[0] // lat

    def to_grid(v, carry):
        block = nn(trig_ref[...], spread[v]).T
        for t in range(lat):
            grid[t, pl.ds(pl.multiple_of(v * SHARD, SHARD), SHARD), :] = block[
                t * SHARD : (t + 1) * SHARD, :
            ]
        return carry

    lax.fori_loop(0, 2 * n_y, to_grid, 0)
    ones = jnp.ones((8, cotpad.shape[0]), jnp.bfloat16)

    def network(t, carry):
        value = grid[t].astype(jnp.bfloat16)
        cotpad[0:lons, :] = cot_ref[pl.ds(pl.multiple_of(t * lons, 16), lons), :]
        cot = cotpad[...]
        bias = biasb[...]
        preact = nn(wt[...], value) + jnp.concatenate([bias, bias], axis=1)
        sigmoid_z = jax.nn.sigmoid(preact)
        activation = (preact * sigmoid_z).astype(jnp.bfloat16)
        grad_act = nt(wout_ref[...], cot)
        grad_pre = (grad_act * sigmoid_z * (1.0 + preact * (1.0 - sigmoid_z))).astype(jnp.bfloat16)
        acc1[...] += nt(value, grad_pre)
        acc2[...] += nn(activation, cot)
        accb1[...] += nt(ones, grad_pre)
        accb2[...] += nn(ones, cot)
        return carry

    lax.fori_loop(0, lat, network, 0)

    chunks = part.shape[0]
    half = chunks // 2
    quarter = chunks // 4
    for q in range(chunks):
        if q < quarter:
            block = acc1[8 * q : 8 * q + 8, :LANES]
        elif q < half:
            block = acc1[8 * (q - quarter) : 8 * (q - quarter) + 8, LANES:]
        else:
            block = acc2[8 * (q - half) : 8 * (q - half) + 8, :]
        part[q, 0:8, :] = block
        if q < 2:
            part[q, 8:9, :] = accb1[0:1, q * LANES : (q + 1) * LANES]
        elif q == 2:
            part[q, 8:9, :] = accb2[0:1, :]
        else:
            part[q, 8:9, :] = jnp.zeros((1, LANES), jnp.float32)

    used = [0]

    def send(src, dst, target):
        slot = used[0]
        used[0] += 1
        return push(src, dst, r_send.at[slot], r_recv.at[slot], target)

    wait_all([send(part.at[pl.ds((1 - core) * half, half)], recv_c, partner)])
    sum_c[...] = part[pl.ds(core * half, half)] + recv_c[...]

    copies = []
    for d in range(1, n_x):
        copies.append(send(sum_c.at[pl.ds(x_peers[d - 1] * n_y, n_y)], recv_x.at[d - 1], x_dev[d - 1]))
    wait_all(copies)
    value = sum_c[pl.ds(x * n_y, n_y)]
    for d in range(1, n_x):
        value = value + recv_x[d - 1]
    sum_x[...] = value

    copies = []
    for d in range(1, n_y):
        copies.append(send(sum_x.at[y_peers[d - 1]], recv_y.at[d - 1], y_dev[d - 1]))
    wait_all(copies)
    value = sum_x[y]
    for d in range(1, n_y):
        value = value + recv_y[d - 1]
    all_z[z] = value

    copies = []
    for d in order:
        copies.append(send(all_z.at[z], all_z.at[z], z_dev[d - 1]))
    wait_all(copies)
    value = all_z[0]
    for s in range(1, n_z):
        value = value + all_z[s]
    mine = (core * n_x + x) * n_y + y
    total[mine] = value

    copies = []
    for d in range(1, n_y):
        copies.append(send(total.at[mine], total.at[mine], y_dev[d - 1]))
    wait_all(copies)
    row = total.at[pl.ds((core * n_x + x) * n_y, n_y)]
    copies = []
    for d in range(1, n_x):
        copies.append(send(row, row, x_dev[d - 1]))
    wait_all(copies)
    side = total.at[pl.ds(core * half, half)]
    wait_all([send(side, side, partner)])
    out_ref[...] = total[...]


def unpack_kernel(total, o1_ref, ob1_ref, o2_ref, ob2_ref):
    chunks = total.shape[0]
    half = chunks // 2
    quarter = chunks // 4
    for q in range(chunks):
        if q < half:
            v = q % quarter
            lo = (q // quarter) * LANES
            o1_ref[4 * v : 4 * v + 4, lo : lo + LANES] = total[q, 0:4, :]
            b = quarter * 4 + 4 * v
            o1_ref[b : b + 4, lo : lo + LANES] = total[q, 4:8, :]
        else:
            o2_ref[8 * (q - half) : 8 * (q - half) + 8, :] = total[q, 0:8, :]
        if q < 2:
            ob1_ref[q : q + 1, :] = total[q, 8:9, :]
        elif q == 2:
            ob2_ref[...] = total[q, 8:9, :]


def gradients(blocks, trig, cot, w_in, b_in, w_out):
    n_z = lax.axis_size("lat")
    n_y = lax.axis_size("lev") // 2
    n_x = lax.axis_size("rep")
    feat, hid = w_in.shape
    chunks = 2 * n_x * n_y
    lat = cot.shape[0] // (LON // (2 * n_y))
    width = trig.shape[0]
    f32 = jnp.float32
    bf16 = jnp.bfloat16
    copies = 2 + 2 * (n_x - 1) + 2 * (n_y - 1) + (n_z - 1)
    vmem = pl.BlockSpec(memory_space=pltpu.VMEM)
    dma = pltpu.SemaphoreType.DMA
    total = pl.pallas_call(
        functools.partial(gradient_kernel, n_x, n_y, n_z),
        out_shape=jax.ShapeDtypeStruct((chunks, ROWS, LANES), f32),
        in_specs=[vmem] * 6,
        out_specs=vmem,
        scratch_shapes=[
            pltpu.VMEM((2 * n_y, n_z * blocks.shape[1], LANES), bf16),
            pltpu.VMEM((lat, feat, width), f32),
            pltpu.VMEM((feat, hid), f32),
            pltpu.VMEM((hid, feat), bf16),
            pltpu.VMEM((hid, LANES), f32),
            pltpu.VMEM((width, LANES), bf16),
            pltpu.VMEM((feat, hid), f32),
            pltpu.VMEM((hid, feat), f32),
            pltpu.VMEM((8, hid), f32),
            pltpu.VMEM((8, feat), f32),
            pltpu.VMEM((chunks, ROWS, LANES), f32),
            pltpu.VMEM((chunks // 2, ROWS, LANES), f32),
            pltpu.VMEM((chunks // 2, ROWS, LANES), f32),
            pltpu.VMEM((n_x - 1, n_y, ROWS, LANES), f32),
            pltpu.VMEM((n_y, ROWS, LANES), f32),
            pltpu.VMEM((n_y - 1, ROWS, LANES), f32),
            pltpu.VMEM((n_z, ROWS, LANES), f32),
            pltpu.VMEM((chunks, ROWS, LANES), f32),
            dma((n_z,)),
            dma((n_z,)),
            dma((GROUPS * n_y,)),
            dma((GROUPS * n_y,)),
            dma((GROUPS * 2 * n_y,)),
            dma((GROUPS * 2 * n_y,)),
            dma((copies,)),
            dma((copies,)),
        ],
        compiler_params=pltpu.CompilerParams(collective_id=0, has_side_effects=True),
        name="gradients",
    )(blocks, trig, cot, w_in, b_in.reshape(1, hid), w_out)
    o1, ob1, o2, ob2 = pl.pallas_call(
        unpack_kernel,
        out_shape=(
            jax.ShapeDtypeStruct((feat, hid), f32),
            jax.ShapeDtypeStruct((2, LANES), f32),
            jax.ShapeDtypeStruct((hid, feat), f32),
            jax.ShapeDtypeStruct((1, LANES), f32),
        ),
        in_specs=[vmem],
        out_specs=(vmem,) * 4,
        name="unpack",
    )(total)
    return o1, ob1.reshape(hid), o2, ob2.reshape(feat)


def body(spectral, legendre, pair_table, weight_in, bias_in, weight_out, cotangent):
    pairs_dev, prow_count, lat_rep = legendre.shape
    lat_count = lax.axis_size("lat")
    lev_count = lax.axis_size("lev")
    lat_index = lax.axis_index("lat")
    lev_index = lax.axis_index("lev")
    lat_dev = lat_rep // lat_count
    lon_dev = LON // lev_count
    local_pair_list = lax.dynamic_slice_in_dim(pair_table, lat_index * pairs_dev, pairs_dev, 0)
    row_ids = jnp.arange(prow_count, dtype=jnp.int32)
    row_count = TRUNCATION_PLUS - local_pair_list[:, 0]
    lower_mask = (row_ids[None, :] < row_count[:, None]).astype(jnp.bfloat16)
    masked = spectral * lower_mask[:, :, None, None, None]
    halves = jnp.stack([masked, spectral - masked], axis=2)
    fourier = jnp.einsum("prl,prwfek->plwefk", legendre, halves, preferred_element_type=jnp.float32)
    fourier = fourier.astype(jnp.bfloat16)
    items = fourier.shape[4] * fourier.shape[5]
    fourier = fourier.reshape(pairs_dev, lat_count, lat_dev, 4, items)
    fourier = fourier.transpose(1, 0, 3, 2, 4).reshape(lat_count, pairs_dev * 4, lat_dev * items)
    blocks = jnp.pad(fourier, ((0, 0), (0, 0), (0, LANES - lat_dev * items)))

    width = -(-lon_dev // LANES) * LANES
    slots = jnp.repeat(pair_table.reshape(-1), 2)
    shift = (jnp.arange(slots.shape[0], dtype=jnp.int32) % 2) * (LON // 4)
    own_lon = lev_index * lon_dev + jnp.arange(width, dtype=jnp.int32)
    product = (slots[None, :] * own_lon[:, None] + shift[None, :]) % LON
    angle = product.astype(jnp.float32) * (2.0 * math.pi / LON)
    trig = (2.0 * jnp.cos(angle)).astype(jnp.bfloat16)
    return gradients(blocks, trig, cotangent.T, weight_in, bias_in, weight_out)


def solution(mesh):
    in_specs = (
        P("lat", None, None, None, "lev"),
        P("lat", None, "rep"),
        P(),
        P(),
        P(),
        P(),
        P(None, ("lat", "lev", "rep")),
    )
    out_specs = (P(), P(), P(), P())
    return jax.shard_map(body, mesh=mesh, in_specs=in_specs, out_specs=out_specs, check_vma=False)
```

time: 175 us -> 143 us (0.82)
  Pallas kernels: 41 us -> 116 us
  waiting for transfers between devices: 48.4 us -> 0 us
  blocking collectives: 33.7 us -> 0 us
  between operations: 14.3 us -> 0.71 us
  matrix products: 14.2 us -> 4.44 us
  local copies, waits for them, and re-layouts: 17 us -> 13.4 us
  other arithmetic: 5.51 us -> 7.55 us
    pallas_call x1 -> x2, Pallas kernels: 41 us -> 116 us  [the longest x1 114 us: gradients(): pl.pallas_call(functools.partial(gradient_kernel, n_x, n_y, n_z), out_sha...]
    all_gather x1 -> x0, waiting for transfers between devices: 48.4 us -> none  [body(): lax.all_gather(transposed, 'lev', axis=0, tiled=True)]
    all_to_all x1 -> x0, blocking collectives: 33.7 us -> none  [body(): lax.all_to_all(fourier, 'lat', split_axis=3, concat_axis=2, tiled=True)]
    dot_general x6 -> x1, matrix products: 14.2 us -> 4.44 us  [body(): jnp.einsum('prl,prwfek->plwefk', legendre, halves, preferred_element_type...]
    unnamed x19 -> x3, local copies, waits for them, and re-layouts: 8.18 us -> 0.14 us
    convert_element_type x0 -> x1, other arithmetic: none -> 6.05 us  [body(): trig = (2.0 * jnp.cos(angle)).astype(jnp.bfloat16)]
    transpose x1, local copies, waits for them, and re-layouts: 0.33 us -> 5.7 us  [body(): fourier.transpose(1, 0, 3, 2, 4)]
    another operation x1 -> x0, other arithmetic: 3.01 us -> none
  transfers between devices with their start and end apart: 1 -> 0, of which waited for: 1 -> 0; matrix products, arithmetic and copies ran while one was open for 2% -> 0% of each run, Pallas kernels for 0% -> 0%
where the time goes in v2:
time: 143 us; the launch traced here: 142 us
  Pallas kernels  116 us (81%)
  local copies, waits for them, and re-layouts  13.4 us (9%)
  other arithmetic  7.55 us (5%)
  matrix products  4.44 us (3%)
    pallas_call x1, Pallas kernels, gradients(): pl.pallas_call(functools.partial(gradient_kernel, n_x, n_y, n_z), out_sha...  114 us
    convert_element_type x1, other arithmetic, body(): trig = (2.0 * jnp.cos(angle)).astype(jnp.bfloat16)  6.05 us
    transpose x1, local copies, waits for them, and re-layouts, body(): fourier.transpose(1, 0, 3, 2, 4)  5.7 us
    dot_general x1, matrix products, body(): jnp.einsum('prl,prwfek->plwefk', legendre, halves, preferred_element_type...  4.44 us
    reshape x1, local copies, waits for them, and re-layouts, body(): fourier = fourier.reshape(pairs_dev, lat_count, lat_dev, 4, items)  3.27 us

profile of v2, /device:TPU:1, one launch (start us, length us, event | category | flops | bytes accessed | tf_op | source)
XLA Modules:
  0.0 142.3 jit_solution(7312491897229198193)
XLA Ops:
  0.6 0.8 constant_dynamic-slice_fusion
  1.4 0.1 fusion.20
  1.5 1.4 multiply_bitcast_fusion
  2.9 4.4 %fusion.13 = bf16[20,240,2,2,2,4]{1,5,3,4,2,0:T(4,128)(2,1)S(1)} fusion(bf16[20,641,240]{2,1,0:T(8,128)(2,1)} %param.8, bf16[20,641,1,2,2,4]{1,5,4,3,2,0:T(4,128)(2,1)S(1)} %get-tuple-element.13, bf16[20,641,1,2,2,4]{1,5,4,3,2,0:T(4,128)(2,1)S(1)} %get-tuple-element.12), kind=kOutput, calls=%fused_computation.13 | convolution fusion | flops 198709760 | bytes 7281280 | tf_op jit(solution)/shard_map/prl,prwfek->plwefk/dot_general | solution.py:366
  7.3 0.1 copy.13
  7.5 3.3 %reshape.64 = bf16[20,16,15,4,8]{2,1,4,3,0:T(8,128)(2,1)S(1)} reshape(bf16[20,240,2,2,2,4]{1,5,4,3,2,0:T(4,128)(2,1)S(1)} %copy.13) | data formatting | bytes 614400 | tf_op jit(solution)/shard_map/reshape | solution.py:369
  10.8 5.7 %copy.14 = bf16[16,20,4,15,8]{0,4,3,2,1:T(8,128)(2,1)} copy(bf16[16,20,4,15,8]{3,0,4,2,1:T(8,128)(2,1)S(1)} %bitcast.27) | data formatting | bytes 614400 | tf_op jit(solution)/shard_map/transpose | solution.py:370
  16.5 0.0 copy-start
  16.5 2.1 %copy.15 = bf16[16,80,120]{2,1,0:T(8,128)(2,1)S(1)} copy(bf16[16,80,120]{0,2,1:T(8,128)(2,1)} %bitcast.28) | data formatting | bytes 614400 | tf_op jit(solution)/shard_map/reshape | solution.py:370
  18.6 0.8 pad.4.f_ref
  19.4 0.0 copy-done
  19.4 0.1 copy.16
  19.5 0.1 reshape.66
  19.7 0.1 broadcast_in_dim.2
  19.8 0.2 mul.54
  20.0 6.0 %fusion.6.trig_ref = bf16[256,1280]{1,0:T(8,128)(2,1)} fusion(s32[1280]{0:T(1024)S(1)} %fusion.21, s32[256]{0:T(256)S(1)} %iota_add_fusion, s32[1280]{0:T(1024)S(1)} %mul.54), kind=kLoop, calls=%fused_computation.7 | loop fusion | flops 3932160 | bytes 666624 | tf_op jit(solution)/shard_map/convert_element_type | solution.py:379
  26.1 114.4 %gradients.1.total = f32[64,9,128]{2,1,0:T(8,128)} custom-call(bf16[16,80,128]{2,1,0:T(8,128)(2,1)} %pad.4.f_ref, bf16[256,1280]{1,0:T(8,128)(2,1)} %fusion.6.trig_ref, bf16[3600,128]{1,0:T(8,128)(2,1)} %bitcast.29, bf16[128,256]{1,0:T(8,128)(2,1)} %win_ref.1, f32[1,256]{1,0:T(1,128)} %bitcast.30, bf16[256,128]{1,0:T(8,128)(2,1)} %wout_ref.1), custom_call_target="tpu_custom_call" | custom-call | tf_op jit(solution)/shard_map/gradients/pallas_call | solution.py:301
  140.5 1.8 %unpack.1 = (f32[128,256]{1,0:T(8,128)}, f32[2,128]{1,0:T(2,128)}, f32[256,128]{1,0:T(8,128)}, f32[1,128]{1,0:T(1,128)}) custom-call(f32[64,9,128]{2,1,0:T(8,128)} %gradients.1.total), custom_call_target="tpu_custom_call" | custom-call | tf_op jit(solution)/shard_map/unpack/pallas_call | solution.py:337
  (3 shorter events, 0.0 us)
Async XLA Ops:
  16.5 2.9 %copy-start = (s32[320,2]{0,1:T(2,128)S(1)}, s32[320,2]{0,1:T(2,128)}, u32[]{:S(2)}) copy-start(s32[320,2]{0,1:T(2,128)} %param.9) | copy-start | bytes 7684

commit v3 on v2

--- a/solution.py
+++ b/solution.py
@@ -54,9 +54,9 @@
 
 def gradient_kernel(
     n_x, n_y, n_z,
-    f_ref, trig_ref, cot_ref, win_ref, bias_ref, wout_ref,
+    f_ref, slots_ref, cot_ref, win_ref, bias_ref, wout_ref,
     out_ref,
-    spread, grid, wperm, wt, biasb, cotpad, acc1, acc2, accb1, accb2,
+    spread, trig, grid, wperm, wt, biasb, cotpad, acc1, acc2, accb1, accb2,
     part, recv_c, sum_c, recv_x, sum_x, recv_y, all_z, total,
     z_send, z_recv, y_send, y_recv, p_send, p_recv, r_send, r_recv,
 ):
@@ -74,6 +74,8 @@
     z_dev = [{"lat": v} for v in z_peers]
     greet([partner] + x_dev + y_dev + z_dev)
 
+    lat = grid.shape[0]
+    lons = cot_ref.shape[0] // lat
     rows = f_ref.shape[1]
     mine_block = spread.at[lev, pl.ds(pl.multiple_of(z * rows, 16), rows)]
     own = pltpu.make_async_copy(f_ref.at[z], mine_block, z_recv.at[z])
@@ -89,6 +91,25 @@
             push(f_ref.at[z_peers[d - 1]], mine_block, z_send.at[d - 1], z_recv.at[z], z_dev[d - 1])
         )
 
+    strip = 16
+
+    def trig_rows(i, carry):
+        rows_at = pl.multiple_of(i * strip, strip)
+        shape = (strip, trig.shape[1])
+        lon = (lax.broadcasted_iota(jnp.int32, shape, 0) + (rows_at + lev * lons)).astype(jnp.float32)
+        shift = lax.rem(lax.broadcasted_iota(jnp.int32, shape, 1), 2).astype(jnp.float32) * (LON // 4)
+        product = slots_ref[...] * lon + shift
+        turns = product * (1.0 / LON)
+        part_turn = (product - jnp.floor(turns) * LON) * (1.0 / LON)
+        angle = (jnp.abs(part_turn - 0.5) - 0.25) * (2.0 * math.pi)
+        square = angle * angle
+        poly = -1.0 / 39916800.0
+        for term in (362880.0, -5040.0, 120.0, -6.0, 1.0):
+            poly = poly * square + 1.0 / term
+        trig[pl.ds(rows_at, strip), :] = (2.0 * angle * poly).astype(jnp.bfloat16)
+        return carry
+
+    lax.fori_loop(0, trig.shape[0] // strip, trig_rows, 0)
     w32 = win_ref[...].astype(jnp.float32)
     levels = w32.shape[0] // SHARD
     for v in range(levels):
@@ -164,11 +185,8 @@
         copy.wait_send()
     wait_all(p_copies)
 
-    lat = grid.shape[0]
-    lons = cot_ref.shape[0] // lat
-
     def to_grid(v, carry):
-        block = nn(trig_ref[...], spread[v]).T
+        block = nn(trig[...], spread[v]).T
         for t in range(lat):
             grid[t, pl.ds(pl.multiple_of(v * SHARD, SHARD), SHARD), :] = block[
                 t * SHARD : (t + 1) * SHARD, :
@@ -285,14 +303,14 @@
             ob2_ref[...] = total[q, 8:9, :]
 
 
-def gradients(blocks, trig, cot, w_in, b_in, w_out):
+def gradients(blocks, slots, cot, w_in, b_in, w_out):
     n_z = lax.axis_size("lat")
     n_y = lax.axis_size("lev") // 2
     n_x = lax.axis_size("rep")
     feat, hid = w_in.shape
     chunks = 2 * n_x * n_y
     lat = cot.shape[0] // (LON // (2 * n_y))
-    width = trig.shape[0]
+    width = -(-(LON // (2 * n_y)) // LANES) * LANES
     f32 = jnp.float32
     bf16 = jnp.bfloat16
     copies = 2 + 2 * (n_x - 1) + 2 * (n_y - 1) + (n_z - 1)
@@ -305,6 +323,7 @@
         out_specs=vmem,
         scratch_shapes=[
             pltpu.VMEM((2 * n_y, n_z * blocks.shape[1], LANES), bf16),
+            pltpu.VMEM((width, slots.shape[1]), bf16),
             pltpu.VMEM((lat, feat, width), f32),
             pltpu.VMEM((feat, hid), f32),
             pltpu.VMEM((hid, feat), bf16),
@@ -333,7 +352,7 @@
         ],
         compiler_params=pltpu.CompilerParams(collective_id=0, has_side_effects=True),
         name="gradients",
-    )(blocks, trig, cot, w_in, b_in.reshape(1, hid), w_out)
+    )(blocks, slots, cot, w_in, b_in.reshape(1, hid), w_out)
     o1, ob1, o2, ob2 = pl.pallas_call(
         unpack_kernel,
         out_shape=(
@@ -349,35 +368,82 @@
     return o1, ob1.reshape(hid), o2, ob2.reshape(feat)
 
 
-def body(spectral, legendre, pair_table, weight_in, bias_in, weight_out, cotangent):
+def legendre_kernel(slots_ref, spec_ref, leg_ref, out_ref, halves, values):
+    step = pl.program_id(0)
+    z = lax.axis_index("lat")
+    count = leg_ref.shape[0]
+    pairs_dev = count * pl.num_programs(0)
+    for b in range(count):
+        pair = step * count + b
+        lower_rows = TRUNCATION_PLUS - slots_ref[4 * (z * pairs_dev + pair)]
+        for e in range(2):
+            for f in range(2):
+                piece = spec_ref[b, f, e].astype(jnp.float32)
+                row_ids = lax.broadcasted_iota(jnp.int32, piece.shape, 1)
+                low = jnp.where(row_ids < lower_rows, piece, 0.0)
+                at = e * SHARD + f * 4
+                halves[at : at + 4, :] = low
+                halves[2 * SHARD + at : 2 * SHARD + at + 4, :] = piece - low
+        result = nn(halves[...].astype(jnp.bfloat16), leg_ref[b])
+        values[pl.ds(pl.multiple_of(pair * 4 * SHARD, 32), 4 * SHARD), :] = result.astype(jnp.bfloat16)
+
+    @pl.when(step == pl.num_programs(0) - 1)
+    def regroup():
+        lat_count = out_ref.shape[0]
+        lat_rep = values.shape[1]
+        lat_dev = lat_rep // lat_count
+        total_rows = values.shape[0]
+        width = 2 * LANES
+        row_item = lax.rem(lax.broadcasted_iota(jnp.int32, (total_rows, width), 0), SHARD)
+        lane_item = lax.rem(lax.broadcasted_iota(jnp.int32, (total_rows, width), 1), SHARD)
+        keep = row_item == lane_item
+        fold = (
+            lax.broadcasted_iota(jnp.int32, (total_rows // SHARD, total_rows), 1) // SHARD
+            == lax.broadcasted_iota(jnp.int32, (total_rows // SHARD, total_rows), 0)
+        ).astype(jnp.bfloat16)
+        lat_row = lax.broadcasted_iota(jnp.int32, (lat_rep, width), 0)
+        lane = lax.broadcasted_iota(jnp.int32, (lat_rep, width), 1)
+        local = lax.rem(lane, LANES) // SHARD
+        for c in range(lat_count // 2):
+            base = (2 * c + lane // LANES) * lat_dev
+            pick = ((lat_row == base + local) & (local < lat_dev)).astype(jnp.bfloat16)
+            wide = nn(values[...], pick)
+            wide = jnp.where(keep, wide, 0.0).astype(jnp.bfloat16)
+            block = nn(fold, wide).astype(jnp.bfloat16)
+            out_ref[2 * c] = block[:, :LANES]
+            out_ref[2 * c + 1] = block[:, LANES:]
+
+
+def fourier_blocks(slots, spectral, legendre):
     pairs_dev, prow_count, lat_rep = legendre.shape
     lat_count = lax.axis_size("lat")
-    lev_count = lax.axis_size("lev")
-    lat_index = lax.axis_index("lat")
-    lev_index = lax.axis_index("lev")
-    lat_dev = lat_rep // lat_count
-    lon_dev = LON // lev_count
-    local_pair_list = lax.dynamic_slice_in_dim(pair_table, lat_index * pairs_dev, pairs_dev, 0)
-    row_ids = jnp.arange(prow_count, dtype=jnp.int32)
-    row_count = TRUNCATION_PLUS - local_pair_list[:, 0]
-    lower_mask = (row_ids[None, :] < row_count[:, None]).astype(jnp.bfloat16)
-    masked = spectral * lower_mask[:, :, None, None, None]
-    halves = jnp.stack([masked, spectral - masked], axis=2)
-    fourier = jnp.einsum("prl,prwfek->plwefk", legendre, halves, preferred_element_type=jnp.float32)
-    fourier = fourier.astype(jnp.bfloat16)
-    items = fourier.shape[4] * fourier.shape[5]
-    fourier = fourier.reshape(pairs_dev, lat_count, lat_dev, 4, items)
-    fourier = fourier.transpose(1, 0, 3, 2, 4).reshape(lat_count, pairs_dev * 4, lat_dev * items)
-    blocks = jnp.pad(fourier, ((0, 0), (0, 0), (0, LANES - lat_dev * items)))
-
-    width = -(-lon_dev // LANES) * LANES
+    view = spectral.transpose(0, 2, 3, 4, 1)
+    count = 4
+    return pl.pallas_call(
+        legendre_kernel,
+        out_shape=jax.ShapeDtypeStruct((lat_count, pairs_dev * 4, LANES), jnp.bfloat16),
+        grid_spec=pltpu.PrefetchScalarGridSpec(
+            num_scalar_prefetch=1,
+            grid=(pairs_dev // count,),
+            in_specs=[
+                pl.BlockSpec((count,) + view.shape[1:], lambda i, s: (i, 0, 0, 0, 0)),
+                pl.BlockSpec((count, prow_count, lat_rep), lambda i, s: (i, 0, 0)),
+            ],
+            out_specs=pl.BlockSpec((lat_count, pairs_dev * 4, LANES), lambda i, s: (0, 0, 0)),
+            scratch_shapes=[
+                pltpu.VMEM((4 * SHARD, prow_count), jnp.float32),
+                pltpu.VMEM((pairs_dev * 4 * SHARD, lat_rep), jnp.bfloat16),
+            ],
+        ),
+        name="fourier_blocks",
+    )(slots, view, legendre)
+
+
+def body(spectral, legendre, pair_table, weight_in, bias_in, weight_out, cotangent):
     slots = jnp.repeat(pair_table.reshape(-1), 2)
-    shift = (jnp.arange(slots.shape[0], dtype=jnp.int32) % 2) * (LON // 4)
-    own_lon = lev_index * lon_dev + jnp.arange(width, dtype=jnp.int32)
-    product = (slots[None, :] * own_lon[:, None] + shift[None, :]) % LON
-    angle = product.astype(jnp.float32) * (2.0 * math.pi / LON)
-    trig = (2.0 * jnp.cos(angle)).astype(jnp.bfloat16)
-    return gradients(blocks, trig, cotangent.T, weight_in, bias_in, weight_out)
+    blocks = fourier_blocks(slots, spectral, legendre)
+    waves = slots.astype(jnp.float32).reshape(1, -1)
+    return gradients(blocks, waves, cotangent.T, weight_in, bias_in, weight_out)
 
 
 def solution(mesh):

time: 143 us -> 129 us (0.902)
  local copies, waits for them, and re-layouts: 13.4 us -> 2.87 us
  Pallas kernels: 116 us -> 125 us
  other arithmetic: 7.55 us -> 0.01 us
  matrix products: 4.44 us -> 0 us
    pallas_call x0 -> x1, Pallas kernels: none -> 9.35 us  [fourier_blocks(): pl.pallas_call(legendre_kernel, out_shape=jax.ShapeDtypeStruct((lat_count...]
    convert_element_type x2 -> x1, other arithmetic: 6.13 us -> 0.01 us  [body(): waves = slots.astype(jnp.float32).reshape(1, -1)]
    transpose x1 -> x0, local copies, waits for them, and re-layouts: 5.7 us -> none  [body(): fourier.transpose(1, 0, 3, 2, 4)]
    reshape x2 -> x0, local copies, waits for them, and re-layouts: 5.37 us -> none  [the longest x1 3.27 us: body(): fourier = fourier.reshape(pairs_dev, lat_count, lat_dev, 4, items)]
    dot_general x1 -> x0, matrix products: 4.44 us -> none  [body(): jnp.einsum('prl,prwfek->plwefk', legendre, halves, preferred_element_type...]
where the time goes in v3:
time: 129 us
  Pallas kernels  125 us (97%)
  local copies, waits for them, and re-layouts  2.87 us (2%)
    pallas_call x1, Pallas kernels, gradients(): pl.pallas_call(functools.partial(gradient_kernel, n_x, n_y, n_z), out_sha...  114 us
    pallas_call x1, Pallas kernels, fourier_blocks(): pl.pallas_call(legendre_kernel, out_shape=jax.ShapeDtypeStruct((lat_count...  9.35 us

profile of v3, /device:TPU:1, one launch (start us, length us, event | category | flops | bytes accessed | tf_op | source)
XLA Modules:
  0.0 128.9 jit_solution(15423212208132686588)
XLA Ops:
  0.6 0.8 copy.11
  1.5 0.1 reshape.35
  1.6 0.1 broadcast_in_dim.5
  1.8 0.8 reshape.36.slots_ref
  2.6 9.4 %fourier_blocks.1.f_ref = bf16[16,80,128]{2,1,0:T(8,128)(2,1)} custom-call(s32[1280]{0:T(1024)} %reshape.36.slots_ref, bf16[20,2,2,4,641]{4,3,2,1,0:T(4,128)(2,1)} %bitcast.6, bf16[20,641,240]{2,1,0:T(8,128)(2,1)} %leg_ref.1), custom_call_target="tpu_custom_call" | custom-call | tf_op jit(solution)/shard_map/fourier_blocks/pallas_call | solution.py:422
  11.9 0.1 broadcast_in_dim.6
  12.1 0.8 convert_element_type.15.slots_ref
  12.9 114.2 %gradients.1.total = f32[64,9,128]{2,1,0:T(8,128)} custom-call(bf16[16,80,128]{2,1,0:T(8,128)(2,1)} %fourier_blocks.1.f_ref, f32[1,1280]{1,0:T(1,128)} %convert_element_type.15.slots_ref, bf16[3600,128]{1,0:T(8,128)(2,1)} %bitcast.5, bf16[128,256]{1,0:T(8,128)(2,1)} %win_ref.1, f32[1,256]{1,0:T(1,128)} %bitcast.7, bf16[256,128]{1,0:T(8,128)(2,1)} %wout_ref.1), custom_call_target="tpu_custom_call" | custom-call | tf_op jit(solution)/shard_map/gradients/pallas_call | solution.py:319
  127.1 1.8 %unpack.1 = (f32[128,256]{1,0:T(8,128)}, f32[2,128]{1,0:T(2,128)}, f32[256,128]{1,0:T(8,128)}, f32[1,128]{1,0:T(1,128)}) custom-call(f32[64,9,128]{2,1,0:T(8,128)} %gradients.1.total), custom_call_target="tpu_custom_call" | custom-call | tf_op jit(solution)/shard_map/unpack/pallas_call | solution.py:356
  (1 shorter events, 0.0 us)

commit v4 on v2

--- a/solution.py
+++ b/solution.py
@@ -16,14 +16,8 @@
 
 
 GROUPS = 4
+PIECES = 5
 SHARD = 8
-
-
-def greet(targets):
-    barrier = pltpu.get_barrier_semaphore()
-    for target in targets:
-        pl.semaphore_signal(barrier, inc=1, device_id=target, device_id_type=MESH)
-    pl.semaphore_wait(barrier, len(targets))
 
 
 def push(src, dst, send_sem, recv_sem, target):
@@ -54,11 +48,11 @@
 
 def gradient_kernel(
     n_x, n_y, n_z,
-    f_ref, trig_ref, cot_ref, win_ref, bias_ref, wout_ref,
+    pairs_smem, spec_ref, leg_hbm, table_ref, cot_ref, win_ref, bias_ref, wout_ref,
     out_ref,
-    spread, grid, wperm, wt, biasb, cotpad, acc1, acc2, accb1, accb2,
+    leg, halves, values, f_ref, spread, waves, trig, dft, grid, wperm, wt, biasb, acc1, acc2,
     part, recv_c, sum_c, recv_x, sum_x, recv_y, all_z, total,
-    z_send, z_recv, y_send, y_recv, p_send, p_recv, r_send, r_recv,
+    l_sem, z_send, z_recv, y_send, y_recv, p_send, p_recv, r_send, r_recv,
 ):
     x = lax.axis_index("rep")
     lev = lax.axis_index("lev")
@@ -72,23 +66,110 @@
     x_dev = [{"rep": v} for v in x_peers]
     y_dev = [{"lev": v * 2 + core} for v in y_peers]
     z_dev = [{"lat": v} for v in z_peers]
-    greet([partner] + x_dev + y_dev + z_dev)
-
+    pieces = []
+    chunk = leg.shape[0] // PIECES
+    for c in range(PIECES):
+        at = pl.ds(c * chunk, chunk)
+        pieces.append(pltpu.make_async_copy(leg_hbm.at[at], leg.at[at], l_sem.at[c]))
+        pieces[c].start()
+    barrier = pltpu.get_barrier_semaphore()
+    targets = [partner] + x_dev + y_dev + z_dev
+    for target in targets:
+        pl.semaphore_signal(barrier, inc=1, device_id=target, device_id_type=MESH)
+
+    lat = grid.shape[0]
+    lons = cot_ref.shape[0] // lat
     rows = f_ref.shape[1]
+    pairs_dev = leg.shape[0]
+    for c in range(PIECES):
+        for b in range(chunk):
+            pair = c * chunk + b
+            lower_rows = TRUNCATION_PLUS - pairs_smem[0, z * pairs_dev + pair]
+            for e in range(2):
+                for f in range(2):
+                    piece = spec_ref[pair, f, e].astype(jnp.float32)
+                    row_ids = lax.broadcasted_iota(jnp.int32, piece.shape, 1)
+                    low = jnp.where(row_ids < lower_rows, piece, 0.0)
+                    at = e * SHARD + f * 4
+                    halves[b, at : at + 4, :] = low
+                    halves[b, 2 * SHARD + at : 2 * SHARD + at + 4, :] = piece - low
+        pieces[c].wait()
+        for b in range(chunk):
+            pair = c * chunk + b
+            result = nn(halves[b].astype(jnp.bfloat16), leg[pair])
+            values[pair * 4 * SHARD : (pair + 1) * 4 * SHARD, :] = result.astype(jnp.bfloat16)
+    pl.semaphore_wait(barrier, len(targets))
+
     mine_block = spread.at[lev, pl.ds(pl.multiple_of(z * rows, 16), rows)]
-    own = pltpu.make_async_copy(f_ref.at[z], mine_block, z_recv.at[z])
-    own.start()
     order = []
     for d in range(1, n_z // 2 + 1):
         order.append(d)
         if d != n_z - d:
             order.append(n_z - d)
+    total_rows, lat_rep = values.shape
+    width = 2 * LANES
+    keep = lax.rem(lax.broadcasted_iota(jnp.int32, (total_rows, width), 0), SHARD) == lax.rem(
+        lax.broadcasted_iota(jnp.int32, (total_rows, width), 1), SHARD
+    )
+    fold = (
+        lax.broadcasted_iota(jnp.int32, (rows, total_rows), 1) // SHARD
+        == lax.broadcasted_iota(jnp.int32, (rows, total_rows), 0)
+    ).astype(jnp.bfloat16)
+    lat_row = lax.broadcasted_iota(jnp.int32, (lat_rep, width), 0)
+    lane = lax.broadcasted_iota(jnp.int32, (lat_rep, width), 1)
+    local = lax.rem(lane, LANES) // SHARD
     z_copies = []
-    for d in order:
-        z_copies.append(
-            push(f_ref.at[z_peers[d - 1]], mine_block, z_send.at[d - 1], z_recv.at[z], z_dev[d - 1])
-        )
-
+    for first, second in [(0, n_z // 2)] + [(d, n_z - d) for d in range(1, n_z // 2)]:
+        to_first = lax.rem(z + first, n_z)
+        to_second = lax.rem(z + second, n_z)
+        base = jnp.where(lane < LANES, to_first * lat, to_second * lat)
+        pick = ((lat_row == base + local) & (local < lat)).astype(jnp.bfloat16)
+        wide = jnp.where(keep, nn(values[...], pick), 0.0).astype(jnp.bfloat16)
+        block = nn(fold, wide).astype(jnp.bfloat16)
+        f_ref[to_first] = block[:, :LANES]
+        f_ref[to_second] = block[:, LANES:]
+        for d, to in ((first, to_first), (second, to_second)):
+            if d == 0:
+                own = pltpu.make_async_copy(f_ref.at[to], mine_block, z_recv.at[z])
+                own.start()
+            else:
+                z_copies.append(
+                    push(f_ref.at[to], mine_block, z_send.at[d - 1], z_recv.at[z], z_dev[d - 1])
+                )
+
+    per = n_z // GROUPS
+    span = per * rows
+    table = table_ref[...].astype(jnp.float32)
+    high = jnp.floor(table * (1.0 / 16.0))
+    digits = jnp.concatenate([high, table - high * 16.0] * 4, axis=0).astype(jnp.bfloat16)
+    shape = (table.shape[1], waves.shape[1])
+    chosen = lax.broadcasted_iota(jnp.int32, shape, 1) // 4 == lax.broadcasted_iota(jnp.int32, shape, 0)
+    found = nn(digits, chosen.astype(jnp.bfloat16))
+    both = found[0:2, :] * 16.0 + found[2:4, :]
+    leading = lax.rem(lax.broadcasted_iota(jnp.int32, (1, waves.shape[1]), 1) // 2, 2) == 0
+    waves[...] = jnp.where(leading, both[0:1, :], both[1:2, :])
+    strip = 16
+
+    for g in range(GROUPS):
+        wave = waves[:, g * span : (g + 1) * span]
+
+        def trig_rows(i, carry, g=g, wave=wave):
+            rows_at = pl.multiple_of(i * strip, strip)
+            shape = (strip, span)
+            lon = (lax.broadcasted_iota(jnp.int32, shape, 0) + (rows_at + lev * lons)).astype(jnp.float32)
+            shift = lax.rem(lax.broadcasted_iota(jnp.int32, shape, 1), 2).astype(jnp.float32) * (LON // 4)
+            product = wave * lon + shift
+            turns = product * (1.0 / LON)
+            part_turn = (product - jnp.floor(turns) * LON) * (1.0 / LON)
+            angle = (jnp.abs(part_turn - 0.5) - 0.25) * (2.0 * math.pi)
+            square = angle * angle
+            poly = -1.0 / 39916800.0
+            for term in (362880.0, -5040.0, 120.0, -6.0, 1.0):
+                poly = poly * square + 1.0 / term
+            trig[g, pl.ds(rows_at, strip), :] = (2.0 * angle * poly).astype(jnp.bfloat16)
+            return carry
+
+        lax.fori_loop(0, trig.shape[1] // strip, trig_rows, 0)
     w32 = win_ref[...].astype(jnp.float32)
     levels = w32.shape[0] // SHARD
     for v in range(levels):
@@ -97,22 +178,18 @@
             b = f * levels * 4 + v * 4
             wperm[a : a + 4, :] = w32[b : b + 4, :]
     wt[...] = wperm[...].T.astype(jnp.bfloat16)
-    biasb[...] = jnp.broadcast_to(bias_ref[...], (LANES, biasb.shape[0])).T
-    cotpad[...] = jnp.zeros(cotpad.shape, cotpad.dtype)
+    bias = jnp.broadcast_to(bias_ref[...], (LANES, biasb.shape[0])).T
+    biasb[...] = jnp.concatenate([bias, bias], axis=1)
     acc1[...] = jnp.zeros(acc1.shape, acc1.dtype)
     acc2[...] = jnp.zeros(acc2.shape, acc2.dtype)
-    accb1[...] = jnp.zeros(accb1.shape, accb1.dtype)
-    accb2[...] = jnp.zeros(accb2.shape, accb2.dtype)
-
-    per = n_z // GROUPS
-    span = per * rows
+
     offsets = [0, 1, GROUPS - 1, 2]
     group = [lax.rem(z // per + o, GROUPS) for o in offsets]
     right = y_dev[0]
     left = y_dev[n_y - 2]
     half_way = n_y // 2
     y_copies = {}
-    p_copies = []
+    p_copies = [[] for b in range(GROUPS)]
 
     def region(origin, b):
         start = pl.multiple_of(group[b] * span, 16)
@@ -128,7 +205,32 @@
     def send_p(b, slot, origin):
         ref = region(origin, b)
         at = b * 2 * n_y + slot
-        p_copies.append(push(ref, ref, p_send.at[at], p_recv.at[at], partner))
+        p_copies[b].append(push(ref, ref, p_send.at[at], p_recv.at[at], partner))
+
+    def add_group(b):
+        start = pl.multiple_of(group[b] * span, 16)
+        waves_of = trig[group[b]]
+
+        def add_pair(v, carry):
+            two = jnp.concatenate(
+                [spread[2 * v, pl.ds(start, span), :], spread[2 * v + 1, pl.ds(start, span), :]], axis=1
+            )
+            value = nn(waves_of, two)
+            if b == 0:
+                dft[v] = value
+            elif b < GROUPS - 1:
+                dft[v] += value
+            else:
+                value = (value + dft[v]).T
+                for h in range(2):
+                    for t in range(lat):
+                        at = h * LANES + t * SHARD
+                        grid[t, pl.ds(pl.multiple_of((2 * v + h) * SHARD, SHARD), SHARD), :] = value[
+                            at : at + SHARD, :
+                        ]
+            return carry
+
+        lax.fori_loop(0, n_y, add_pair, 0)
 
     last = [[half_way if b % 2 == 0 else half_way - 1, half_way if b % 2 else half_way - 1] for b in range(GROUPS)]
     for tick in range(GROUPS + half_way):
@@ -158,43 +260,36 @@
                     if step < last[b][way]:
                         send_y(b, way, step + 1, origin)
                     send_p(b, 1 + way * half_way + step - 1, origin)
+        done = tick - half_way
+        if done >= 0:
+            for copy in p_copies[done]:
+                copy.wait_recv()
+            add_group(done)
     for copy in z_copies:
         copy.wait_send()
     for copy in y_copies.values():
         copy.wait_send()
-    wait_all(p_copies)
-
-    lat = grid.shape[0]
-    lons = cot_ref.shape[0] // lat
-
-    def to_grid(v, carry):
-        block = nn(trig_ref[...], spread[v]).T
-        for t in range(lat):
-            grid[t, pl.ds(pl.multiple_of(v * SHARD, SHARD), SHARD), :] = block[
-                t * SHARD : (t + 1) * SHARD, :
-            ]
-        return carry
-
-    lax.fori_loop(0, 2 * n_y, to_grid, 0)
-    ones = jnp.ones((8, cotpad.shape[0]), jnp.bfloat16)
+    for copies in p_copies:
+        for copy in copies:
+            copy.wait_send()
+
+    width = grid.shape[2]
+    ones = jnp.ones((16, width), jnp.bfloat16)
+    blank = jnp.zeros((width - lons, LANES), jnp.bfloat16)
 
     def network(t, carry):
         value = grid[t].astype(jnp.bfloat16)
-        cotpad[0:lons, :] = cot_ref[pl.ds(pl.multiple_of(t * lons, 16), lons), :]
-        cot = cotpad[...]
-        bias = biasb[...]
-        preact = nn(wt[...], value) + jnp.concatenate([bias, bias], axis=1)
+        cot = jnp.concatenate([cot_ref[pl.ds(pl.multiple_of(t * lons, 16), lons), :], blank], axis=0)
+        preact = nn(wt[...], value) + biasb[...]
         sigmoid_z = jax.nn.sigmoid(preact)
         activation = (preact * sigmoid_z).astype(jnp.bfloat16)
         grad_act = nt(wout_ref[...], cot)
         grad_pre = (grad_act * sigmoid_z * (1.0 + preact * (1.0 - sigmoid_z))).astype(jnp.bfloat16)
-        acc1[...] += nt(value, grad_pre)
-        acc2[...] += nn(activation, cot)
-        accb1[...] += nt(ones, grad_pre)
-        accb2[...] += nn(ones, cot)
+        acc1[...] += nt(jnp.concatenate([value, ones], axis=0), grad_pre)
+        acc2[...] += nn(jnp.concatenate([activation, ones], axis=0), cot)
         return carry
 
-    lax.fori_loop(0, lat, network, 0)
+    lax.fori_loop(0, lat, network, 0, unroll=3)
 
     chunks = part.shape[0]
     half = chunks // 2
@@ -208,9 +303,9 @@
             block = acc2[8 * (q - half) : 8 * (q - half) + 8, :]
         part[q, 0:8, :] = block
         if q < 2:
-            part[q, 8:9, :] = accb1[0:1, q * LANES : (q + 1) * LANES]
+            part[q, 8:9, :] = acc1[2 * quarter * 4 : 2 * quarter * 4 + 1, q * LANES : (q + 1) * LANES]
         elif q == 2:
-            part[q, 8:9, :] = accb2[0:1, :]
+            part[q, 8:9, :] = acc2[half * 8 : half * 8 + 1, :]
         else:
             part[q, 8:9, :] = jnp.zeros((1, LANES), jnp.float32)
 
@@ -285,14 +380,18 @@
             ob2_ref[...] = total[q, 8:9, :]
 
 
-def gradients(blocks, trig, cot, w_in, b_in, w_out):
+def gradients(pairs, spec, leg, cot, w_in, b_in, w_out):
     n_z = lax.axis_size("lat")
     n_y = lax.axis_size("lev") // 2
     n_x = lax.axis_size("rep")
+    pairs_dev, prow_count, lat_rep = leg.shape
     feat, hid = w_in.shape
     chunks = 2 * n_x * n_y
-    lat = cot.shape[0] // (LON // (2 * n_y))
-    width = trig.shape[0]
+    lons = LON // (2 * n_y)
+    lat = cot.shape[0] // lons
+    width = -(-lons // LANES) * LANES
+    rows = pairs_dev * 4
+    depth = n_z * rows
     f32 = jnp.float32
     bf16 = jnp.bfloat16
     copies = 2 + 2 * (n_x - 1) + 2 * (n_y - 1) + (n_z - 1)
@@ -301,19 +400,23 @@
     total = pl.pallas_call(
         functools.partial(gradient_kernel, n_x, n_y, n_z),
         out_shape=jax.ShapeDtypeStruct((chunks, ROWS, LANES), f32),
-        in_specs=[vmem] * 6,
+        in_specs=[pl.BlockSpec(memory_space=pltpu.SMEM), vmem, pl.BlockSpec(memory_space=pl.ANY)] + [vmem] * 5,
         out_specs=vmem,
         scratch_shapes=[
-            pltpu.VMEM((2 * n_y, n_z * blocks.shape[1], LANES), bf16),
+            pltpu.VMEM((pairs_dev, prow_count, lat_rep), bf16),
+            pltpu.VMEM((pairs_dev // PIECES, 4 * SHARD, prow_count), f32),
+            pltpu.VMEM((rows * SHARD, lat_rep), bf16),
+            pltpu.VMEM((n_z, rows, LANES), bf16),
+            pltpu.VMEM((2 * n_y, depth, LANES), bf16),
+            pltpu.VMEM((1, depth), f32),
+            pltpu.VMEM((GROUPS, width, depth // GROUPS), bf16),
+            pltpu.VMEM((n_y, width, 2 * LANES), f32),
             pltpu.VMEM((lat, feat, width), f32),
             pltpu.VMEM((feat, hid), f32),
             pltpu.VMEM((hid, feat), bf16),
-            pltpu.VMEM((hid, LANES), f32),
-            pltpu.VMEM((width, LANES), bf16),
-            pltpu.VMEM((feat, hid), f32),
-            pltpu.VMEM((hid, feat), f32),
-            pltpu.VMEM((8, hid), f32),
-            pltpu.VMEM((8, feat), f32),
+            pltpu.VMEM((hid, width), f32),
+            pltpu.VMEM((feat + 16, hid), f32),
+            pltpu.VMEM((hid + 16, feat), f32),
             pltpu.VMEM((chunks, ROWS, LANES), f32),
             pltpu.VMEM((chunks // 2, ROWS, LANES), f32),
             pltpu.VMEM((chunks // 2, ROWS, LANES), f32),
@@ -322,6 +425,7 @@
             pltpu.VMEM((n_y - 1, ROWS, LANES), f32),
             pltpu.VMEM((n_z, ROWS, LANES), f32),
             pltpu.VMEM((chunks, ROWS, LANES), f32),
+            dma((PIECES,)),
             dma((n_z,)),
             dma((n_z,)),
             dma((GROUPS * n_y,)),
@@ -333,7 +437,7 @@
         ],
         compiler_params=pltpu.CompilerParams(collective_id=0, has_side_effects=True),
         name="gradients",
-    )(blocks, trig, cot, w_in, b_in.reshape(1, hid), w_out)
+    )(pairs, spec, leg, pairs, cot, w_in, b_in.reshape(1, hid), w_out)
     o1, ob1, o2, ob2 = pl.pallas_call(
         unpack_kernel,
         out_shape=(
@@ -350,34 +454,8 @@
 
 
 def body(spectral, legendre, pair_table, weight_in, bias_in, weight_out, cotangent):
-    pairs_dev, prow_count, lat_rep = legendre.shape
-    lat_count = lax.axis_size("lat")
-    lev_count = lax.axis_size("lev")
-    lat_index = lax.axis_index("lat")
-    lev_index = lax.axis_index("lev")
-    lat_dev = lat_rep // lat_count
-    lon_dev = LON // lev_count
-    local_pair_list = lax.dynamic_slice_in_dim(pair_table, lat_index * pairs_dev, pairs_dev, 0)
-    row_ids = jnp.arange(prow_count, dtype=jnp.int32)
-    row_count = TRUNCATION_PLUS - local_pair_list[:, 0]
-    lower_mask = (row_ids[None, :] < row_count[:, None]).astype(jnp.bfloat16)
-    masked = spectral * lower_mask[:, :, None, None, None]
-    halves = jnp.stack([masked, spectral - masked], axis=2)
-    fourier = jnp.einsum("prl,prwfek->plwefk", legendre, halves, preferred_element_type=jnp.float32)
-    fourier = fourier.astype(jnp.bfloat16)
-    items = fourier.shape[4] * fourier.shape[5]
-    fourier = fourier.reshape(pairs_dev, lat_count, lat_dev, 4, items)
-    fourier = fourier.transpose(1, 0, 3, 2, 4).reshape(lat_count, pairs_dev * 4, lat_dev * items)
-    blocks = jnp.pad(fourier, ((0, 0), (0, 0), (0, LANES - lat_dev * items)))
-
-    width = -(-lon_dev // LANES) * LANES
-    slots = jnp.repeat(pair_table.reshape(-1), 2)
-    shift = (jnp.arange(slots.shape[0], dtype=jnp.int32) % 2) * (LON // 4)
-    own_lon = lev_index * lon_dev + jnp.arange(width, dtype=jnp.int32)
-    product = (slots[None, :] * own_lon[:, None] + shift[None, :]) % LON
-    angle = product.astype(jnp.float32) * (2.0 * math.pi / LON)
-    trig = (2.0 * jnp.cos(angle)).astype(jnp.bfloat16)
-    return gradients(blocks, trig, cotangent.T, weight_in, bias_in, weight_out)
+    view = spectral.transpose(0, 2, 3, 4, 1)
+    return gradients(pair_table.T, view, legendre, cotangent.T, weight_in, bias_in, weight_out)
 
 
 def solution(mesh):

time: 143 us -> 114 us (0.80)
  local copies, waits for them, and re-layouts: 13.4 us -> 0 us
  other arithmetic: 7.55 us -> 0 us
  matrix products: 4.44 us -> 0 us
  Pallas kernels: 116 us -> 113 us
    convert_element_type x2 -> x0, other arithmetic: 6.13 us -> none  [the longest x1 6.05 us: body(): trig = (2.0 * jnp.cos(angle)).astype(jnp.bfloat16)]
    transpose x1 -> x0, local copies, waits for them, and re-layouts: 5.7 us -> none  [body(): fourier.transpose(1, 0, 3, 2, 4)]
    reshape x3 -> x0, local copies, waits for them, and re-layouts: 5.51 us -> none  [the longest x1 3.27 us: body(): fourier = fourier.reshape(pairs_dev, lat_count, lat_dev, 4, items)]
    dot_general x1 -> x0, matrix products: 4.44 us -> none  [body(): jnp.einsum('prl,prwfek->plwefk', legendre, halves, preferred_element_type...]
    pallas_call x1, Pallas kernels: 114 us -> 111 us  [gradients(): pl.pallas_call(functools.partial(gradient_kernel, n_x, n_y, n_z), out_sha...]
where the time goes in v4:
time: 114 us
  Pallas kernels  113 us (99%)
    pallas_call x1, Pallas kernels, gradients(): pl.pallas_call(functools.partial(gradient_kernel, n_x, n_y, n_z), out_sha...  111 us

profile of v4, /device:TPU:1, one launch (start us, length us, event | category | flops | bytes accessed | tf_op | source)
XLA Modules:
  0.0 113.6 jit_solution(2499634304562059124)
XLA Ops:
  0.6 111.2 %gradients.1.total = f32[64,9,128]{2,1,0:T(8,128)} custom-call(s32[2,320]{1,0:T(2,128)} %bitcast.8, bf16[20,2,2,4,641]{4,3,2,1,0:T(4,128)(2,1)} %bitcast.7, bf16[20,641,240]{2,1,0:T(8,128)(2,1)} %leg_hbm.1, s32[2,320]{1,0:T(2,128)} %bitcast.9, bf16[3600,128]{1,0:T(8,128)(2,1)} %bitcast.6, bf16[128,256]{1,0:T(8,128)(2,1)} %win_ref.1, f32[1,256]{1,0:T(1,128)} %bitcast.10, ...), custom_call_target="tpu_custom_call" | custom-call | tf_op jit(solution)/shard_map/gradients/pallas_call | solution.py:400
  111.8 1.8 %unpack.1 = (f32[128,256]{1,0:T(8,128)}, f32[2,128]{1,0:T(2,128)}, f32[256,128]{1,0:T(8,128)}, f32[1,128]{1,0:T(1,128)}) custom-call(f32[64,9,128]{2,1,0:T(8,128)} %gradients.1.total), custom_call_target="tpu_custom_call" | custom-call | tf_op jit(solution)/shard_map/unpack/pallas_call | solution.py:441

commit v5 on v4

--- a/solution.py
+++ b/solution.py
@@ -11,7 +11,7 @@
 TRUNCATION_PLUS = 1280
 LON = 3840
 LANES = 128
-ROWS = 9
+ROWS = 16
 MESH = pl.DeviceIdType.MESH
 
 
@@ -36,6 +36,10 @@
 def wait_all(copies):
     for copy in copies:
         copy.wait()
+
+
+def wide(a):
+    return a.astype(jnp.float32)
 
 
 def nt(a, b):
@@ -124,8 +128,8 @@
         to_second = lax.rem(z + second, n_z)
         base = jnp.where(lane < LANES, to_first * lat, to_second * lat)
         pick = ((lat_row == base + local) & (local < lat)).astype(jnp.bfloat16)
-        wide = jnp.where(keep, nn(values[...], pick), 0.0).astype(jnp.bfloat16)
-        block = nn(fold, wide).astype(jnp.bfloat16)
+        spaced = jnp.where(keep, nn(values[...], pick), 0.0).astype(jnp.bfloat16)
+        block = nn(fold, spaced).astype(jnp.bfloat16)
         f_ref[to_first] = block[:, :LANES]
         f_ref[to_second] = block[:, LANES:]
         for d, to in ((first, to_first), (second, to_second)):
@@ -301,13 +305,13 @@
             block = acc1[8 * (q - quarter) : 8 * (q - quarter) + 8, LANES:]
         else:
             block = acc2[8 * (q - half) : 8 * (q - half) + 8, :]
-        part[q, 0:8, :] = block
         if q < 2:
-            part[q, 8:9, :] = acc1[2 * quarter * 4 : 2 * quarter * 4 + 1, q * LANES : (q + 1) * LANES]
+            tail = acc1[8 * quarter : 8 * quarter + 8, q * LANES : (q + 1) * LANES]
         elif q == 2:
-            part[q, 8:9, :] = acc2[half * 8 : half * 8 + 1, :]
+            tail = acc2[8 * half : 8 * half + 8, :]
         else:
-            part[q, 8:9, :] = jnp.zeros((1, LANES), jnp.float32)
+            tail = jnp.zeros((8, LANES), jnp.float32)
+        part[q] = jnp.concatenate([block, tail], axis=0).astype(part.dtype)
 
     used = [0]
 
@@ -317,35 +321,35 @@
         return push(src, dst, r_send.at[slot], r_recv.at[slot], target)
 
     wait_all([send(part.at[pl.ds((1 - core) * half, half)], recv_c, partner)])
-    sum_c[...] = part[pl.ds(core * half, half)] + recv_c[...]
+    sum_c[...] = (wide(part[pl.ds(core * half, half)]) + wide(recv_c[...])).astype(sum_c.dtype)
 
     copies = []
     for d in range(1, n_x):
         copies.append(send(sum_c.at[pl.ds(x_peers[d - 1] * n_y, n_y)], recv_x.at[d - 1], x_dev[d - 1]))
     wait_all(copies)
-    value = sum_c[pl.ds(x * n_y, n_y)]
+    value = wide(sum_c[pl.ds(x * n_y, n_y)])
     for d in range(1, n_x):
-        value = value + recv_x[d - 1]
-    sum_x[...] = value
+        value = value + wide(recv_x[d - 1])
+    sum_x[...] = value.astype(sum_x.dtype)
 
     copies = []
     for d in range(1, n_y):
         copies.append(send(sum_x.at[y_peers[d - 1]], recv_y.at[d - 1], y_dev[d - 1]))
     wait_all(copies)
-    value = sum_x[y]
+    value = wide(sum_x[y])
     for d in range(1, n_y):
-        value = value + recv_y[d - 1]
-    all_z[z] = value
+        value = value + wide(recv_y[d - 1])
+    all_z[z] = value.astype(all_z.dtype)
 
     copies = []
     for d in order:
         copies.append(send(all_z.at[z], all_z.at[z], z_dev[d - 1]))
     wait_all(copies)
-    value = all_z[0]
+    value = wide(all_z[0])
     for s in range(1, n_z):
-        value = value + all_z[s]
+        value = value + wide(all_z[s])
     mine = (core * n_x + x) * n_y + y
-    total[mine] = value
+    total[mine] = value.astype(total.dtype)
 
     copies = []
     for d in range(1, n_y):
@@ -366,18 +370,19 @@
     half = chunks // 2
     quarter = chunks // 4
     for q in range(chunks):
+        block = wide(total[q])
         if q < half:
             v = q % quarter
             lo = (q // quarter) * LANES
-            o1_ref[4 * v : 4 * v + 4, lo : lo + LANES] = total[q, 0:4, :]
+            o1_ref[4 * v : 4 * v + 4, lo : lo + LANES] = block[0:4, :]
             b = quarter * 4 + 4 * v
-            o1_ref[b : b + 4, lo : lo + LANES] = total[q, 4:8, :]
+            o1_ref[b : b + 4, lo : lo + LANES] = block[4:8, :]
         else:
-            o2_ref[8 * (q - half) : 8 * (q - half) + 8, :] = total[q, 0:8, :]
+            o2_ref[8 * (q - half) : 8 * (q - half) + 8, :] = block[0:8, :]
         if q < 2:
-            ob1_ref[q : q + 1, :] = total[q, 8:9, :]
+            ob1_ref[q : q + 1, :] = block[8:9, :]
         elif q == 2:
-            ob2_ref[...] = total[q, 8:9, :]
+            ob2_ref[...] = block[8:9, :]
 
 
 def gradients(pairs, spec, leg, cot, w_in, b_in, w_out):
@@ -399,7 +404,7 @@
     dma = pltpu.SemaphoreType.DMA
     total = pl.pallas_call(
         functools.partial(gradient_kernel, n_x, n_y, n_z),
-        out_shape=jax.ShapeDtypeStruct((chunks, ROWS, LANES), f32),
+        out_shape=jax.ShapeDtypeStruct((chunks, ROWS, LANES), bf16),
         in_specs=[pl.BlockSpec(memory_space=pltpu.SMEM), vmem, pl.BlockSpec(memory_space=pl.ANY)] + [vmem] * 5,
         out_specs=vmem,
         scratch_shapes=[
@@ -417,14 +422,14 @@
             pltpu.VMEM((hid, width), f32),
             pltpu.VMEM((feat + 16, hid), f32),
             pltpu.VMEM((hid + 16, feat), f32),
-            pltpu.VMEM((chunks, ROWS, LANES), f32),
-            pltpu.VMEM((chunks // 2, ROWS, LANES), f32),
-            pltpu.VMEM((chunks // 2, ROWS, LANES), f32),
-            pltpu.VMEM((n_x - 1, n_y, ROWS, LANES), f32),
-            pltpu.VMEM((n_y, ROWS, LANES), f32),
-            pltpu.VMEM((n_y - 1, ROWS, LANES), f32),
-            pltpu.VMEM((n_z, ROWS, LANES), f32),
-            pltpu.VMEM((chunks, ROWS, LANES), f32),
+            pltpu.VMEM((chunks, ROWS, LANES), bf16),
+            pltpu.VMEM((chunks // 2, ROWS, LANES), bf16),
+            pltpu.VMEM((chunks // 2, ROWS, LANES), bf16),
+            pltpu.VMEM((n_x - 1, n_y, ROWS, LANES), bf16),
+            pltpu.VMEM((n_y, ROWS, LANES), bf16),
+            pltpu.VMEM((n_y - 1, ROWS, LANES), bf16),
+            pltpu.VMEM((n_z, ROWS, LANES), bf16),
+            pltpu.VMEM((chunks, ROWS, LANES), bf16),
             dma((PIECES,)),
             dma((n_z,)),
             dma((n_z,)),

time: 114 us -> 113 us (level)
  no operation moved by 1% of the time
where the time goes in v5:
time: 113 us
  Pallas kernels  112 us (99%)
    pallas_call x1, Pallas kernels, gradients(): pl.pallas_call(functools.partial(gradient_kernel, n_x, n_y, n_z), out_sha...  111 us

profile of v5, /device:TPU:1, one launch (start us, length us, event | category | flops | bytes accessed | tf_op | source)
XLA Modules:
  0.0 112.9 jit_solution(8627448588489162180)
XLA Ops:
  0.6 110.6 %gradients.1.total = bf16[64,16,128]{2,1,0:T(8,128)(2,1)} custom-call(s32[2,320]{1,0:T(2,128)} %bitcast.8, bf16[20,2,2,4,641]{4,3,2,1,0:T(4,128)(2,1)} %bitcast.7, bf16[20,641,240]{2,1,0:T(8,128)(2,1)} %leg_hbm.1, s32[2,320]{1,0:T(2,128)} %bitcast.9, bf16[3600,128]{1,0:T(8,128)(2,1)} %bitcast.6, bf16[128,256]{1,0:T(8,128)(2,1)} %win_ref.1, ...), custom_call_target="tpu_custom_call" | custom-call | tf_op jit(solution)/shard_map/gradients/pallas_call | solution.py:405
  111.2 1.7 %unpack.1 = (f32[128,256]{1,0:T(8,128)}, f32[2,128]{1,0:T(2,128)}, f32[256,128]{1,0:T(8,128)}, f32[1,128]{1,0:T(1,128)}) custom-call(bf16[64,16,128]{2,1,0:T(8,128)(2,1)} %gradients.1.total), custom_call_target="tpu_custom_call" | custom-call | tf_op jit(solution)/shard_map/unpack/pallas_call | solution.py:446
